TPU v7x, 32 devices: a whole 2x2x4 slice. The times are simulated.
32 devices in a mesh: wide: 8 (over z, y), narrow: 4 (over x, core).
Axes of the slice: x: 2, y: 2, z: 4, core: 2. Of those that a mesh axis runs over, the one named last changes fastest.
Arguments:
- tokens: bfloat16 [32, 256, 1024], P(('wide', 'narrow')), may hold values from -6 to 6
- segment_ids: int32 [32, 256], P(('wide', 'narrow')), may hold values from 0 to 3, never falling along the last dimension, each value on 1 to 128 neighbouring positions
- routed_index: int32 [32, 32], P(('wide', 'narrow')), may hold values from 0 to 255, as said below
- out_grad: bfloat16 [32, 256, 1024], P(('wide', 'narrow')), may hold values from -6 to 6
- dense_attn_gain: bfloat16 [1024], P('wide'), may hold values from 0.5 to 1.5
- dense_qkv: bfloat16 [1024, 3072], P('wide'), may hold values from -0.1875 to 0.1875
- dense_proj: bfloat16 [1024, 1024], P('wide'), may hold values from -0.75 to 0.75
- dense_mlp_gain: bfloat16 [1024], P('wide'), may hold values from 0.5 to 1.5
- dense_up: bfloat16 [1024, 4096], P('wide'), may hold values from -0.1875 to 0.1875
- dense_down: bfloat16 [4096, 1024], P('wide'), may hold values from -0.09375 to 0.09375
- routed_attn_gain: bfloat16 [1024], P('wide'), may hold values from 0.5 to 1.5
- routed_qkv: bfloat16 [1024, 3072], P('wide'), may hold values from -0.1875 to 0.1875
- routed_proj: bfloat16 [1024, 1024], P('wide'), may hold values from -0.75 to 0.75
- routed_mlp_gain: bfloat16 [1024], P('wide'), may hold values from 0.5 to 1.5
- routed_up: bfloat16 [1024, 4096], P('wide'), may hold values from -0.1875 to 0.1875
- routed_down: bfloat16 [4096, 1024], P('wide'), may hold values from -0.09375 to 0.09375
- router_vector: bfloat16 [1024], replicated, may hold values from -0.1875 to 0.1875
Outputs:
- result: bfloat16 [32, 256, 1024], P(('wide', 'narrow'))
- input_grad: bfloat16 [32, 256, 1024], P(('wide', 'narrow'))
- grad_dense_attn_gain: float32 [1024], P('wide')
- grad_dense_qkv: float32 [1024, 3072], P('wide')
- grad_dense_proj: float32 [1024, 1024], P('wide')
- grad_dense_mlp_gain: float32 [1024], P('wide')
- grad_dense_up: float32 [1024, 4096], P('wide')
- grad_dense_down: float32 [4096, 1024], P('wide')
- grad_routed_attn_gain: float32 [1024], P('wide')
- grad_routed_qkv: float32 [1024, 3072], P('wide')
- grad_routed_proj: float32 [1024, 1024], P('wide')
- grad_routed_mlp_gain: float32 [1024], P('wide')
- grad_routed_up: float32 [1024, 4096], P('wide')
- grad_routed_down: float32 [4096, 1024], P('wide')
- router_grad: float32 [1024], replicated
Inputs may be any that keep to these rules, and one draw needn't show every extreme that they name: `routed_index`: each row holds 32 distinct positions of its sequence in increasing order.
All inputs are finite; a program needn't handle non-finite values.
Results may differ from a plain program's by a relative error of at most 0.022.
Values may be sent and summed in bfloat16 or wider, within the bound.
No kernel may reach another device: no remote copies, remote signals or barrier semaphores. Data moves between devices by JAX's collectives and lax.ppermute only.
A program may use at most 256 MiB of HBM per device.

v0:
```python
import functools

import jax
import jax.numpy as jnp
from jax import lax
from jax.experimental import pallas as pl
from jax.experimental.pallas import tpu as pltpu
from jax.sharding import PartitionSpec as P

HEADS = 16
EPS = 1e-06
NEG = -1e30
HIGH = lax.Precision.HIGHEST
LOW = jnp.bfloat16
F32 = jnp.float32
I32 = jnp.int32
VMEM_SPEC = pl.BlockSpec(memory_space=pltpu.VMEM)
SMEM_SPEC = pl.BlockSpec(memory_space=pltpu.SMEM)
ANY_SPEC = pl.BlockSpec(memory_space=pl.ANY)


def dot_rows(left, right):
    return jnp.dot(left, right, preferred_element_type=F32)


def dot_cross(left, right):
    return lax.dot_general(left, right, (((0,), (0,)), ((), ())), preferred_element_type=F32)


def dot_back(left, right):
    return lax.dot_general(left, right, (((1,), (1,)), ((), ())), preferred_element_type=F32)


def bits_of(size):
    found = []
    bit = size // 2
    while bit >= 1:
        found.append(bit)
        bit //= 2
    return found


def xor_blocks(array, index, blocks, axis):
    size = array.shape[axis] // blocks
    for bit in bits_of(blocks):
        parts = [
            lax.slice_in_dim(array, k * size, (k + 1) * size, axis=axis) for k in range(blocks)
        ]
        swapped = jnp.concatenate([parts[k ^ bit] for k in range(blocks)], axis=axis)
        array = jnp.where((index & bit) != 0, swapped, array)
    return array


class Links:
    def __init__(self, sizes):
        self.sizes = sizes

    def swap(self, array, axis, bit):
        return lax.ppermute(array, axis, [(i, i ^ bit) for i in range(self.sizes[axis])])

    def gather(self, local, axis, order):
        for bit in order:
            local = jnp.concatenate([local, self.swap(local, axis, bit)], 0)
        return local


class Gather:
    def __init__(self, links, piece, order):
        self.links = links
        self.arrays = [piece]
        self.offsets = [[0]]
        self.todo = [(order[0], None)]
        made = 1
        for bit in order[1:]:
            self.todo += [(bit, i) for i in range(made)]
            made *= 2

    def next(self, count=1):
        for bit, at in self.todo[:count]:
            got = self.links.swap(self.arrays[at or 0], "wide", bit)
            offsets = [k ^ bit for k in self.offsets[at or 0]]
            if at is None:
                self.arrays = [jnp.concatenate([self.arrays[0], got], 0)]
                self.offsets = [self.offsets[0] + offsets]
            else:
                self.arrays.append(got)
                self.offsets.append(offsets)
        self.todo = self.todo[count:]

    def finish(self):
        self.next(len(self.todo))
        return list(zip(self.offsets, self.arrays))


class Scatter:
    def __init__(self, links, columns, index, order):
        self.links = links
        self.index = index
        self.bits = bits_of(links.sizes["wide"])
        self.left = list(order[::-1])
        lead = (2,) * len(self.bits)
        size = links.sizes["wide"]
        self.base = [c.reshape(lead + (c.shape[0] // size, c.shape[1])) for c in columns]
        self.got = None
        self.at = None
        self.mine = None

    @property
    def arrays(self):
        return [self.base] if self.got is None else [self.base, self.got]

    @arrays.setter
    def arrays(self, values):
        self.base = values[0]
        if self.got is not None:
            self.got = values[1]

    def value(self):
        def pick(c):
            return lax.dynamic_index_in_dim(c, self.mine, self.at, keepdims=False)

        if self.got is None:
            return jnp.concatenate(self.base, -1) if len(self.base) > 1 else self.base[0]
        kept = jnp.concatenate([pick(c) for c in self.base], -1)
        return (kept.astype(F32) + self.got.astype(F32)).astype(LOW)

    def next(self):
        if not self.left:
            return
        bit = self.left.pop(0)
        at = self.bits.index(bit)
        mine = jnp.where((self.index & bit) != 0, 1, 0).astype(I32)
        if self.got is not None:
            self.base = [self.value()]
        send = jnp.concatenate(
            [lax.dynamic_index_in_dim(c, 1 - mine, at, keepdims=False) for c in self.base], -1
        )
        self.bits.pop(at)
        self.at, self.mine = at, mine
        self.got = self.links.swap(send, "wide", bit)

    def finish(self):
        while self.left:
            self.next()
        return self.value()


def sync(movers, *values):
    held = lax.optimization_barrier(([m.arrays for m in movers], values))
    for mover, arrays in zip(movers, held[0]):
        mover.arrays = arrays
    return held[1]


def order_of(order):
    offsets = [0]
    for bit in order:
        offsets = offsets + [k ^ bit for k in offsets]
    return offsets


def pack(index, narrow, shards, layouts):
    def kernel(index_ref, *refs):
        ins, outs, sems = refs[: len(shards)], refs[len(shards) : -1], refs[-1]
        at = index_ref[0]
        copies = []

        def add(source, target):
            copies.append(pltpu.make_async_copy(source, target, sems.at[len(copies)]))

        for (out, members), out_ref in zip(layouts, outs):
            low = 0
            for member, blocks, width in members:
                source = ins[member]
                if blocks is None:
                    size = source.shape[0] // narrow
                    add(source.at[pl.ds(pl.multiple_of(at * size, size), size), :], out_ref.at[0])
                    continue
                for block in range(blocks):
                    start = pl.multiple_of((block * narrow + at) * width, width)
                    add(source.at[:, pl.ds(start, width)], out_ref.at[0, :, low : low + width])
                    low += width
        for copy in copies:
            copy.start()
        for copy in copies:
            copy.wait()

    count = sum(1 if m[1] is None else m[1] for _, members in layouts for m in members)
    return pl.pallas_call(
        kernel,
        out_shape=[jax.ShapeDtypeStruct((1,) + shape, LOW) for shape, _ in layouts],
        in_specs=[SMEM_SPEC] + [ANY_SPEC] * len(shards),
        out_specs=[VMEM_SPEC] * len(layouts),
        scratch_shapes=[pltpu.SemaphoreType.DMA((count,))],
    )(index.reshape(1), *shards)


def assemble(parts, index, widths):
    count = sum(len(ks) for ks, _ in parts)
    own = parts[0][1].shape[1]
    spans = []
    start = 0
    for width in widths:
        spans.append((start, start + width))
        start += width

    def kernel(index_ref, *refs):
        ins, outs, sems = refs[: len(parts)], refs[len(parts) : -1], refs[-1]
        copies = []
        for (ks, _), source in zip(parts, ins):
            for j, k in enumerate(ks):
                row = pl.multiple_of((index_ref[0] ^ k) * own, own)
                for (low, high), out in zip(spans, outs):
                    copies.append(
                        pltpu.make_async_copy(
                            source.at[j, :, low:high],
                            out.at[pl.ds(row, own), :],
                            sems.at[len(copies)],
                        )
                    )
        for copy in copies:
            copy.start()
        for copy in copies:
            copy.wait()

    return pl.pallas_call(
        kernel,
        out_shape=[jax.ShapeDtypeStruct((count * own, width), LOW) for width in widths],
        in_specs=[SMEM_SPEC] + [ANY_SPEC] * len(parts),
        out_specs=[VMEM_SPEC] * len(widths),
        scratch_shapes=[pltpu.SemaphoreType.DMA((count * len(widths),))],
    )(index.reshape(1), *[a for _, a in parts])


def head_columns(ref, part, head, heads, width):
    start = (part * heads + head) * width
    return ref[:, start : start + width]


def head_prob(query, key, bias):
    scores = dot_back(query, key) + bias
    lifted = jnp.exp(scores - jnp.max(scores, -1, keepdims=True))
    return lifted / jnp.sum(lifted, -1, keepdims=True)


def attend_kernel(heads, combined_ref, bias_ref, out_ref):
    width = out_ref.shape[1] // heads
    bias = bias_ref[0]
    outs = []
    for head in range(heads):
        query = head_columns(combined_ref, 0, head, heads, width) * LOW(width**-0.5)
        key = head_columns(combined_ref, 1, head, heads, width)
        val = head_columns(combined_ref, 2, head, heads, width)
        prob = head_prob(query, key, bias).astype(LOW)
        outs.append(dot_rows(prob, val).astype(LOW))
    out_ref[...] = jnp.concatenate(outs, 1)


def attend_back_kernel(heads, combined_ref, grad_ref, bias_ref, out_ref):
    width = grad_ref.shape[1] // heads
    scale = width**-0.5
    bias = bias_ref[0]
    outs = [[], [], []]
    for head in range(heads):
        query = head_columns(combined_ref, 0, head, heads, width) * LOW(scale)
        key = head_columns(combined_ref, 1, head, heads, width)
        val = head_columns(combined_ref, 2, head, heads, width)
        grad = head_columns(grad_ref, 0, head, heads, width)
        prob = head_prob(query, key, bias)
        prob_grad = dot_back(grad, val)
        inner = jnp.sum(prob * prob_grad, -1, keepdims=True)
        score_grad = (prob * (prob_grad - inner)).astype(LOW)
        outs[0].append((dot_rows(score_grad, key) * scale).astype(LOW))
        outs[1].append(dot_cross(score_grad, query).astype(LOW))
        outs[2].append(dot_cross(prob.astype(LOW), grad).astype(LOW))
    out_ref[...] = jnp.concatenate(outs[0] + outs[1] + outs[2], 1)


def attend_call(heads, combined, bias, out_grad=None):
    groups, rows, _ = bias.shape
    third = combined.shape[1] // 3

    def rows_spec(cols):
        return pl.BlockSpec((rows, cols), lambda i: (i, 0))

    bias_spec = pl.BlockSpec((1, rows, rows), lambda i: (i, 0, 0))
    total = groups * rows
    if out_grad is None:
        return pl.pallas_call(
            functools.partial(attend_kernel, heads),
            grid=(groups,),
            out_shape=jax.ShapeDtypeStruct((total, third), LOW),
            in_specs=[rows_spec(3 * third), bias_spec],
            out_specs=rows_spec(third),
        )(combined, bias)
    return pl.pallas_call(
        functools.partial(attend_back_kernel, heads),
        grid=(groups,),
        out_shape=jax.ShapeDtypeStruct((total, 3 * third), LOW),
        in_specs=[rows_spec(3 * third), rows_spec(third), bias_spec],
        out_specs=rows_spec(3 * third),
    )(combined, out_grad, bias)


def place(gathered, index, order, plans):
    count, _, own, _ = gathered.shape

    def kernel(index_ref, in_ref, *out_refs):
        for j in range(count):
            offset = index_ref[0] ^ j
            entry = 0
            for position, k in enumerate(order):
                entry = jnp.where(offset == k, position, entry)
            for (group, first, pieces, chunk), out_ref in zip(plans, out_refs):
                if chunk is None:
                    out_ref[j * own : (j + 1) * own, :] = in_ref[entry, group].astype(F32)
                    continue
                for p in range(pieces):
                    at = (p * count + j) * chunk
                    low = first + p * chunk
                    out_ref[:, at : at + chunk] = in_ref[
                        entry, group, :, low : low + chunk
                    ].astype(F32)

    shapes = [
        (count * own, gathered.shape[3]) if chunk is None else (own, pieces * count * chunk)
        for _, _, pieces, chunk in plans
    ]
    return pl.pallas_call(
        kernel,
        out_shape=[jax.ShapeDtypeStruct(shape, F32) for shape in shapes],
        in_specs=[SMEM_SPEC, VMEM_SPEC],
        out_specs=[VMEM_SPEC] * len(plans),
    )(index.reshape(1), gathered)


def norm_stats(values):
    return lax.rsqrt(jnp.mean(values * values, -1, keepdims=True) + EPS)


def norm_back(values, scale, gain, grad):
    weighted = grad * gain
    inner = jnp.mean(weighted * values, -1, keepdims=True)
    return scale * (weighted - values * (scale * scale) * inner)


def gelu_parts(v):
    root = 0.7978845608028654
    inner = jnp.tanh(root * (v + 0.044715 * v * v * v))
    value = 0.5 * v * (1.0 + inner)
    slope = 0.5 * (1.0 + inner) + 0.5 * v * (1.0 - inner * inner) * root * (
        1.0 + 3.0 * 0.044715 * v * v
    )
    return value, slope


def make_device(wide, narrow):
    wide_bits = bits_of(wide)
    narrow_bits = bits_of(narrow)
    order_a = list(wide_bits)
    order_b = wide_bits[:-2] + wide_bits[-2:][::-1]
    near = order_of(narrow_bits)

    def per_device(
        tokens,
        segment_ids,
        routed_index,
        out_grad,
        dense_attn_gain,
        dense_qkv,
        dense_proj,
        dense_mlp_gain,
        dense_up,
        dense_down,
        routed_attn_gain,
        routed_qkv,
        routed_proj,
        routed_mlp_gain,
        routed_up,
        routed_down,
        router_vector,
    ):
        links = Links({"wide": wide, "narrow": narrow})
        w = lax.axis_index("wide").astype(I32)
        n = lax.axis_index("narrow").astype(I32)
        inputs = tokens[0].astype(F32)
        rows, width = inputs.shape
        segments = segment_ids[0]
        chosen = routed_index[0]
        cap = chosen.shape[0]
        heads = HEADS // narrow
        own = width // wide
        ffn = dense_up.shape[1]
        part = width // narrow
        unit = ffn // (wide * narrow)

        def pieces_of(qkv, proj, up, down):
            if unit % 128 == 0:
                return pack(
                    n,
                    narrow,
                    [qkv, proj, up, down],
                    [
                        ((own, 4 * part), [(0, 3, part), (1, 1, part)]),
                        ((own, ffn // narrow), [(2, wide, unit)]),
                        ((unit, width), [(3, None, None)]),
                    ],
                )
            mixed = jnp.concatenate(
                [qkv.reshape(own, 3, narrow, part), proj.reshape(own, 1, narrow, part)], 1
            )

            def pick(array, axis):
                return lax.dynamic_index_in_dim(array, n, axis, keepdims=False)

            return (
                pick(mixed, 2).reshape(1, own, 4 * part),
                pick(up.reshape(own, wide, narrow, unit), 2).reshape(1, own, -1),
                pick(down.reshape(narrow, unit, width), 0)[None],
            )

        def swap_blocks(array, axis):
            got = []
            for k in range(narrow):
                block = lax.dynamic_slice_in_dim(array, (n ^ k) * part, part, axis)
                got.append(block if k == 0 else links.swap(block, "narrow", k))
            return got

        def open_attn(parts):
            qkv_full, proj_cols = assemble(parts, w, (3 * part, part))
            got = swap_blocks(proj_cols, 0)
            return qkv_full, xor_blocks(jnp.concatenate(got, 1), n, narrow, 1)

        def proj_columns(proj_grad):
            return xor_blocks(jnp.concatenate(swap_blocks(proj_grad, 1), 0), n, narrow, 0)

        def flat(array):
            return array.reshape(-1, array.shape[-1])

        def share_far(local):
            return links.gather(local[None], "narrow", narrow_bits[:-1])

        def share_core(first):
            return links.swap(first, "narrow", narrow_bits[-1])

        def share(local):
            first = share_far(local)
            return jnp.concatenate([first, share_core(first)], 0)

        def total_core(first, second):
            got = share_core(second)
            keep = first.reshape(narrow // 2, -1, width)
            return keep.astype(F32) + got.reshape(narrow // 2, -1, width).astype(F32)

        def total_far(sums):
            for bit in narrow_bits[:-1][::-1]:
                half = sums.shape[0] // 2
                got = links.swap(sums[half:].astype(LOW), "narrow", bit)
                sums = sums[:half] + got.astype(F32)
            return sums[0]

        def total(whole):
            half = whole.shape[0] // 2
            return total_far(total_core(whole[:half], whole[half:]))

        def rows_low(chunk, weight):
            return dot_rows(chunk, weight).astype(LOW)

        def back_low(chunk, weight):
            return dot_back(chunk, weight).astype(LOW)

        def cross(lefts, rights):
            out = dot_cross(lefts[0], rights[0])
            for left, right in zip(lefts[1:], rights[1:]):
                out = out + dot_cross(left, right)
            return out.astype(LOW)

        def normed_of(values, scale, gain):
            return (values * scale * gain).astype(LOW)

        def active_of(hidden_pre):
            return gelu_parts(hidden_pre)[0].astype(LOW)

        def pre_grad_of(hidden_pre, grad, down):
            return (gelu_parts(hidden_pre)[1] * dot_back(grad, down)).astype(LOW)

        def gain_grad(weight, grad, gain):
            return jnp.sum(weight.astype(F32) * grad, -1) / gain.astype(F32)

        piece_a, piece_u, piece_d = pieces_of(dense_qkv, dense_proj, dense_up, dense_down)
        get_a = Gather(links, piece_a, order_a)
        get_u = Gather(links, piece_u, order_a)
        get_d = Gather(links, piece_d, order_a)
        get_a.next()
        gains = jnp.stack([dense_attn_gain, dense_mlp_gain, routed_attn_gain, routed_mlp_gain])
        gains = links.gather(gains[None], "wide", order_a)
        marks = share(jnp.concatenate([segments, chosen, jnp.take(segments, chosen)]))
        scale_0 = norm_stats(inputs)
        pieces_r = pieces_of(routed_qkv, routed_proj, routed_up, routed_down)
        full_ra, full_ru, full_rd = [
            lax.all_gather(piece[0], "wide", axis=0, tiled=True) for piece in pieces_r
        ]
        moving = [get_a, get_u, get_d]
        gains, marks, scale_0 = sync(moving, gains, marks, scale_0)

        get_a.next()
        get_u.next()
        spread = order_of(order_a)
        places = jnp.array([spread.index(k) for k in range(wide)], I32)
        gains = jnp.take(gains, places[w ^ jnp.arange(wide, dtype=I32)], axis=0)
        gains = gains.transpose(1, 0, 2).reshape(4, width).astype(F32)
        normed_0 = [share_far(normed_of(inputs, scale_0, gains[0]))]
        gains, normed_0, marks = sync(moving, gains, normed_0, marks)

        get_a.next(2)
        get_u.next()
        get_d.next()
        normed_0.append(share_core(normed_0[0]))
        normed_0 = [flat(c) for c in normed_0]
        seg_all = marks[:, :rows]
        pos_r = marks[:, rows : rows + cap]
        seg_r = marks[:, rows + cap :].reshape(-1)
        where_r, of_r = pos_r.reshape(-1), jnp.repeat(jnp.arange(narrow, dtype=I32), cap)
        pos = jnp.arange(rows, dtype=I32)
        allowed = (pos[None, None, :] <= pos[None, :, None]) & (
            seg_all[:, None, :] == seg_all[:, :, None]
        )
        bias_0 = jnp.where(allowed, 0.0, NEG).astype(F32)
        bias_0 = [bias_0[: narrow // 2], bias_0[narrow // 2 :]]
        allowed = (where_r[None, :] <= where_r[:, None]) & (seg_r[None, :] == seg_r[:, None])
        allowed = allowed & (of_r[None, :] == of_r[:, None])
        bias_r = jnp.where(allowed, 0.0, NEG).astype(F32)[None]
        hits_all = (pos[None, :, None] == pos_r[:, None, :]).astype(LOW)
        normed_0, bias_0 = sync(moving, normed_0, bias_0)

        moving = [get_u, get_d]
        get_u.next(2)
        get_d.next()
        qkv_d, proj_d = open_attn(get_a.finish())
        combined_0 = [rows_low(c, qkv_d) for c in normed_0]
        attended_0 = [attend_call(heads, c, b) for c, b in zip(combined_0, bias_0)]
        second = rows_low(attended_0[1], proj_d)
        sums = total_core(rows_low(attended_0[0], proj_d), second)
        attended_0, proj_d, qkv_d, sums = sync(moving, attended_0, proj_d, qkv_d, sums)

        get_d.next(2)
        hidden = inputs + total_far(sums)
        scale_1 = norm_stats(hidden)
        normed_1 = [share_far(normed_of(hidden, scale_1, gains[1]))]
        up_d = assemble(get_u.finish(), w, (ffn // narrow,))[0]
        normed_1.append(share_core(normed_1[0]))
        normed_1 = [flat(c) for c in normed_1]
        pre_1 = [dot_rows(c, up_d) for c in normed_1]
        active_1 = [active_of(c) for c in pre_1]
        active_1, pre_1, up_d = sync([get_d], active_1, pre_1, up_d)
        down_d = assemble(get_d.finish(), w, (width,))[0]
        second = rows_low(active_1[1], down_d)
        sums = total_core(rows_low(active_1[0], down_d), second)
        middle = hidden + total_far(sums)

        selected = jnp.take(middle, chosen, axis=0)
        route_vec = router_vector.astype(F32)
        rate = jax.nn.sigmoid(jnp.dot(selected, route_vec, precision=HIGH))
        scale_2 = norm_stats(selected)
        normed_2 = flat(share(normed_of(selected, scale_2, gains[2])))
        qkv_r, proj_r = full_ra[:, : 3 * part], swap_blocks(full_ra[:, 3 * part :], 0)
        proj_r = xor_blocks(jnp.concatenate(proj_r, 1), n, narrow, 1)
        combined_2 = rows_low(normed_2, qkv_r)
        attended_2 = attend_call(heads, combined_2, bias_r)
        routed_att = total(rows_low(attended_2, proj_r))
        result_grad = out_grad[0]
        picked_grad = jnp.take(result_grad, chosen, axis=0).astype(F32)
        change_grad = rate[:, None] * picked_grad
        grad_3 = flat(share(change_grad.astype(LOW)))

        scale_3 = norm_stats(selected + routed_att)
        normed_3 = flat(share(normed_of(selected + routed_att, scale_3, gains[3])))
        grad_far = share_far(result_grad)
        grad_share = [grad_far, share_core(grad_far)]
        up_r, down_r = full_ru, full_rd
        pre_3 = dot_rows(normed_3, up_r)
        active_3 = active_of(pre_3)
        routed_out = rows_low(active_3, down_r)

        pre_grad_3 = pre_grad_of(pre_3, grad_3, down_r)
        normed_part = back_low(pre_grad_3, up_r)
        both_r = jnp.concatenate(
            [cross([normed_3], [pre_grad_3]), cross([active_3], [grad_3])], 1
        )
        both_r, normed_part, routed_out, grad_share = sync(
            [], both_r, normed_part, routed_out, grad_share
        )
        shard_r = lax.psum_scatter(both_r, "wide", scatter_dimension=0, tiled=True)

        after = selected + routed_att
        after_grad = norm_back(after, scale_3, gains[3], total(normed_part))
        grad_2 = flat(share((change_grad + after_grad).astype(LOW)))
        combined_grad_2 = attend_call(heads, combined_2, bias_r, back_low(grad_2, proj_r))
        normed_part = back_low(combined_grad_2, qkv_r)
        change = routed_att + total(routed_out)
        normed_part, change, grad_2, combined_grad_2 = sync(
            [], normed_part, change, grad_2, combined_grad_2
        )

        rate_grad = jnp.sum(picked_grad * change, -1)
        logit_grad = rate_grad * rate * (1.0 - rate)
        att_in_grad = norm_back(selected, scale_2, gains[2], total(normed_part))
        selected_grad = after_grad + att_in_grad + logit_grad[:, None] * route_vec[None, :]
        fresh = share((picked_grad + selected_grad).astype(LOW))
        proj_grad = proj_columns(cross([attended_2], [grad_2]))
        qkv_grad = cross([normed_2], [combined_grad_2])
        put_ra = Scatter(links, [qkv_grad, proj_grad], w, order_a)
        router_total = jnp.dot(logit_grad, selected, precision=HIGH)
        hops = [("narrow", bit) for bit in narrow_bits] + [("wide", bit) for bit in wide_bits]

        def hop(value):
            if hops:
                value = value + links.swap(value, *hops.pop(0))
            return value

        router_total = hop(router_total)
        fresh, selected_grad, router_total = sync(
            [put_ra], fresh, selected_grad, router_total
        )

        put_ra.next()
        placed = jnp.einsum("sqk,skd->sqd", hits_all, fresh, preferred_element_type=F32)
        taken = jnp.any(hits_all != 0, -1, keepdims=True)
        half = narrow // 2
        grad_1 = [
            flat(jnp.where(taken[i * half : (i + 1) * half],
                           placed[i * half : (i + 1) * half].astype(LOW), base))
            for i, base in enumerate(grad_share)
        ]
        pre_grad_1 = [pre_grad_of(h, g, down_d) for h, g in zip(pre_1, grad_1)]
        second = back_low(pre_grad_1[1], up_d)
        sums = total_core(back_low(pre_grad_1[0], up_d), second)
        put_d = Scatter(links, [cross(active_1, grad_1)], w, order_a)
        router_total = hop(router_total)
        moving = [put_ra, put_d]
        sums, pre_grad_1, router_total = sync(moving, sums, pre_grad_1, router_total)

        put_d.next()
        put_ra.next()
        hits = (pos[:, None] == chosen[None, :]).astype(F32)
        middle_grad = result_grad.astype(F32) + jnp.dot(hits, selected_grad, precision=HIGH)
        hidden_grad = middle_grad + norm_back(hidden, scale_1, gains[1], total_far(sums))
        put_u = Scatter(links, [cross(normed_1, pre_grad_1)], w, order_a)
        grad_0 = [share_far(hidden_grad.astype(LOW))]
        router_total = hop(router_total)
        moving = [put_ra, put_d, put_u]
        grad_0, hidden_grad, router_total = sync(moving, grad_0, hidden_grad, router_total)

        put_u.next()
        put_d.next()
        put_ra.next()
        grad_0.append(share_core(grad_0[0]))
        grad_0 = [flat(c) for c in grad_0]
        combined_grad_0 = [
            attend_call(heads, c, b, back_low(g, proj_d))
            for c, b, g in zip(combined_0, bias_0, grad_0)
        ]
        second = back_low(combined_grad_0[1], qkv_d)
        sums = total_core(back_low(combined_grad_0[0], qkv_d), second)
        router_total = hop(router_total)
        sums, combined_grad_0, grad_0, router_total = sync(
            moving, sums, combined_grad_0, grad_0, router_total
        )

        put_u.next()
        put_d.next()
        proj_grad = proj_columns(cross(attended_0, grad_0))
        qkv_grad = cross(normed_0, combined_grad_0)
        put_a = Scatter(links, [qkv_grad, proj_grad], w, order_a)
        input_part = norm_back(inputs, scale_0, gains[0], total_far(sums))
        input_total = (hidden_grad + input_part).astype(LOW)
        router_total = hop(router_total)
        moving = [put_ra, put_d, put_u, put_a]
        input_total, router_total = sync(moving, input_total, router_total)

        def far(shards):
            return links.gather(jnp.stack(shards)[None], "narrow", narrow_bits[:-1])

        put_a.next()
        put_u.next()
        added = jnp.dot(hits, rate[:, None] * change, precision=HIGH)
        result = (middle + added).astype(LOW)
        while hops:
            router_total = hop(router_total)
        result, router_total = sync([put_a, put_u, put_d], result, router_total)

        put_a.next()
        far_d = far([put_u.finish(), put_d.finish()])
        (far_d,) = sync([put_a], far_d)

        put_a.next()
        ffn_part = ffn // narrow
        far_r = far([shard_r[:, :ffn_part], shard_r[:, ffn_part:], put_ra.finish()])
        done_d = jnp.concatenate([far_d, share_core(far_d)], 0)
        done_d, far_r = sync([put_a], done_d, far_r)
        done_r = jnp.concatenate([far_r, share_core(far_r)], 0)
        far_a = far([put_a.finish()])
        done_a = jnp.concatenate([far_a, share_core(far_a)], 0)

        plans_f = [(0, 0, wide, unit), (1, 0, 1, None)]

        def plans_a(group):
            return [(group, 0, 3, part), (group, 3 * part, 1, part)]

        out_up_r, out_down_r, out_qkv_r, out_proj_r = place(done_r, n, near, plans_f + plans_a(2))
        out_up, out_down = place(done_d, n, near, plans_f)
        out_qkv, out_proj = place(done_a, n, near, plans_a(0))
        return (
            result[None],
            input_total[None],
            gain_grad(dense_qkv, out_qkv, dense_attn_gain),
            out_qkv,
            out_proj,
            gain_grad(dense_up, out_up, dense_mlp_gain),
            out_up,
            out_down,
            gain_grad(routed_qkv, out_qkv_r, routed_attn_gain),
            out_qkv_r,
            out_proj_r,
            gain_grad(routed_up, out_up_r, routed_mlp_gain),
            out_up_r,
            out_down_r,
            router_total,
        )

    return per_device


def solution(mesh):
    both = P(("wide", "narrow"))
    wide = P("wide")
    weights = (wide,) * 6
    return jax.shard_map(
        make_device(mesh.shape["wide"], mesh.shape["narrow"]),
        mesh=mesh,
        in_specs=(both, both, both, both) + weights + weights + (P(),),
        out_specs=(both, both) + weights + weights + (P(),),
        check_vma=False,
    )
```

profile of v0, /device:TPU:0, one launch (start us, length us, event | category | flops | bytes accessed | tf_op | source)
XLA Modules:
  0.0 581.5 jit_solution(8752238104490827638)
XLA Ops:
  8.0 4.1 collective-permute-start.1
  28.9 4.8 collective-permute-done
  38.5 11.4 %collective-permute-done.7 = bf16[1,128,1024]{2,1,0:T(8,128)(2,1)S(1)} collective-permute-done((bf16[1,128,1024]{2,1,0:T(8,128)(2,1)S(1)}, bf16[1,128,1024]{2,1,0:T(8,128)(2,1)S(1)}, u32[]{:S(2)}, u32[]{:S(2)}) %collective-permute-start.7) | collective-permute-done | bytes 262176 | tf_op jit(solution)/shard_map/ppermute | solution.py:59
  50.1 5.6 collective-permute-done.6.refs_1_
  64.5 12.3 %collective-permute-done.12 = bf16[1,128,1024]{2,1,0:T(8,128)(2,1)S(1)} collective-permute-done((bf16[1,128,1024]{2,1,0:T(8,128)(2,1)S(1)}, bf16[1,128,1024]{2,1,0:T(8,128)(2,1)S(1)}, u32[]{:S(2)}, u32[]{:S(2)}) %collective-permute-start.12) | collective-permute-done | bytes 262176 | tf_op jit(solution)/shard_map/ppermute | solution.py:59
  77.6 9.9 %collective-permute-done.10.refs_3_ = bf16[2,128,1024]{2,1,0:T(8,128)(2,1)S(1)} collective-permute-done((bf16[2,128,1024]{2,1,0:T(8,128)(2,1)}, bf16[2,128,1024]{2,1,0:T(8,128)(2,1)S(1)}, u32[]{:S(2)}, u32[]{:S(2)}) %collective-permute-start.10) | collective-permute-done | bytes 524320 | tf_op jit(solution)/shard_map/ppermute | solution.py:59
  89.6 3.4 shard_map.290
  96.4 3.3 convolution_convert_fusion.12.combined_ref
  99.8 4.1 shard_map.292
  110.9 4.1 shard_map.291
  116.7 4.4 collective-permute-done.14.refs_2_
  121.1 10.8 %collective-permute-done.15.refs_3_ = bf16[2,128,1024]{2,1,0:T(8,128)(2,1)} collective-permute-done((bf16[2,128,1024]{2,1,0:T(8,128)(2,1)S(1)}, bf16[2,128,1024]{2,1,0:T(8,128)(2,1)}, u32[]{:S(2)}, u32[]{:S(2)}) %collective-permute-start.15) | collective-permute-done | bytes 524320 | tf_op jit(solution)/shard_map/ppermute | solution.py:59
  134.5 11.0 %collective-permute-done.21 = bf16[1,256,1024]{2,1,0:T(8,128)(2,1)S(1)} collective-permute-done((bf16[1,256,1024]{2,1,0:T(8,128)(2,1)S(1)}, bf16[1,256,1024]{2,1,0:T(8,128)(2,1)S(1)}, u32[]{:S(2)}, u32[]{:S(2)}) %collective-permute-start.21) | collective-permute-done | bytes 524320 | tf_op jit(solution)/shard_map/ppermute | solution.py:59
  149.4 11.2 %collective-permute-done.24 = bf16[1,256,1024]{2,1,0:T(8,128)(2,1)S(1)} collective-permute-done((bf16[1,256,1024]{2,1,0:T(8,128)(2,1)S(1)}, bf16[1,256,1024]{2,1,0:T(8,128)(2,1)S(1)}, u32[]{:S(2)}, u32[]{:S(2)}) %collective-permute-start.24) | collective-permute-done | bytes 524320 | tf_op jit(solution)/shard_map/ppermute | solution.py:59
  165.9 5.0 fusion.4
  170.8 4.1 fusion.9
  175.0 9.3 %collective-permute-done.22.refs_2_ = bf16[2,128,1024]{2,1,0:T(8,128)(2,1)} collective-permute-done((bf16[2,128,1024]{2,1,0:T(8,128)(2,1)}, bf16[2,128,1024]{2,1,0:T(8,128)(2,1)}, u32[]{:S(2)}, u32[]{:S(2)}) %collective-permute-start.22) | collective-permute-done | bytes 524320 | tf_op jit(solution)/shard_map/ppermute | solution.py:59
  184.3 11.1 %collective-permute-done.23.refs_3_ = bf16[2,128,1024]{2,1,0:T(8,128)(2,1)} collective-permute-done((bf16[2,128,1024]{2,1,0:T(8,128)(2,1)}, bf16[2,128,1024]{2,1,0:T(8,128)(2,1)}, u32[]{:S(2)}, u32[]{:S(2)}) %collective-permute-start.23) | collective-permute-done | bytes 524320 | tf_op jit(solution)/shard_map/ppermute | solution.py:59
  195.4 2.9 shard_map.294
  198.3 3.8 convolution_convert_fusion.8
  202.3 3.2 convolution_convert_fusion.9
  214.7 8.4 %collective-permute-done.27 = bf16[1,256,1024]{2,1,0:T(8,128)(2,1)S(1)} collective-permute-done((bf16[1,256,1024]{2,1,0:T(8,128)(2,1)}, bf16[1,256,1024]{2,1,0:T(8,128)(2,1)S(1)}, u32[]{:S(2)}, u32[]{:S(2)}) %collective-permute-start.27) | collective-permute-done | bytes 524320 | tf_op jit(solution)/shard_map/ppermute | solution.py:59
  234.9 3.1 shard_map.296
  251.3 4.8 collective-permute-done.34
  262.1 3.5 collective-permute-done.37
  267.9 2.9 fusion.32
  287.7 3.0 collective-permute-done.42
  300.3 3.7 shard_map.297
  308.3 9.3 %collective-permute-start.48 = (bf16[256,256]{1,0:T(8,128)(2,1)S(1)}, bf16[256,256]{1,0:T(8,128)(2,1)S(1)}, u32[]{:S(2)}, u32[]{:S(2)}) collective-permute-start(bf16[256,256]{1,0:T(8,128)(2,1)S(1)} %get-tuple-element.302), channel_id=1, source_target_pairs={{0,3},{1,2},{2,1},{3,0},{4,7},{5,6},{6,5},{7,4},{8,11},{9,10},{10,... | collective-permute-start | bytes 393224 | tf_op jit(solution)/shard_map/ppermute | solution.py:59
  345.7 10.4 %collective-permute-done.55 = bf16[2,2,128,1024]{3,2,0,1:T(8,128)(2,1)S(1)} collective-permute-done((bf16[2,2,128,1024]{3,2,0,1:T(8,128)(2,1)S(1)}, bf16[2,2,128,1024]{3,2,0,1:T(8,128)(2,1)S(1)}, u32[]{:S(2)}, u32[]{:S(2)}) %collective-permute-start.55) | collective-permute-done | bytes 1048608 | tf_op jit(solution)/shard_map/ppermute | solution.py:59
  362.3 9.7 %collective-permute-done.60 = bf16[1,256,1024]{2,1,0:T(8,128)(2,1)S(1)} collective-permute-done((bf16[1,256,1024]{2,1,0:T(8,128)(2,1)S(1)}, bf16[1,256,1024]{2,1,0:T(8,128)(2,1)S(1)}, u32[]{:S(2)}, u32[]{:S(2)}) %collective-permute-start.60) | collective-permute-done | bytes 524320 | tf_op jit(solution)/shard_map/ppermute | solution.py:59
  381.2 6.2 %collective-permute-done.61 = bf16[1,256,1024]{2,1,0:T(8,128)(2,1)S(1)} collective-permute-done((bf16[1,256,1024]{2,1,0:T(8,128)(2,1)S(1)}, bf16[1,256,1024]{2,1,0:T(8,128)(2,1)S(1)}, u32[]{:S(2)}, u32[]{:S(2)}) %collective-permute-start.61) | collective-permute-done | bytes 524320 | tf_op jit(solution)/shard_map/ppermute | solution.py:59
  393.8 6.9 %shard_map.299 = bf16[512,768]{1,0:T(8,128)(2,1)} custom-call(bf16[512,768]{1,0:T(8,128)(2,1)} %convolution_convert_fusion.12.combined_ref, bf16[512,256]{1,0:T(8,128)(2,1)} %convolution_convert_fusion.15.grad_ref, f32[2,256,256]{2,1,0:T(8,128)} %get-tuple-element.169.bias_ref), custom_call_target="tpu_custom_call" | custom-call | tf_op jit(solution)/shard_map/pallas_call | solution.py:296
  400.7 3.8 convolution_convert_fusion.4
  404.9 7.3 %shard_map.298 = bf16[512,768]{1,0:T(8,128)(2,1)} custom-call(bf16[512,768]{1,0:T(8,128)(2,1)} %convolution_convert_fusion.13.combined_ref, bf16[512,256]{1,0:T(8,128)(2,1)} %convolution_convert_fusion.16.grad_ref, f32[2,256,256]{2,1,0:T(8,128)} %get-tuple-element.167.bias_ref), custom_call_target="tpu_custom_call" | custom-call | tf_op jit(solution)/shard_map/pallas_call | solution.py:296
  420.9 18.5 %collective-permute-done.63 = bf16[128,1024]{1,0:T(8,128)(2,1)S(1)} collective-permute-done((bf16[128,1024]{1,0:T(8,128)(2,1)S(1)}, bf16[128,1024]{1,0:T(8,128)(2,1)S(1)}, u32[]{:S(2)}, u32[]{:S(2)}) %collective-permute-start.63) | collective-permute-done | bytes 262176 | tf_op jit(solution)/shard_map/ppermute | solution.py:59
  439.3 6.9 %collective-permute-done.64 = bf16[2,128,1024]{2,1,0:T(8,128)(2,1)S(1)} collective-permute-done((bf16[2,128,1024]{2,1,0:T(8,128)(2,1)S(1)}, bf16[2,128,1024]{2,1,0:T(8,128)(2,1)S(1)}, u32[]{:S(2)}, u32[]{:S(2)}) %collective-permute-start.64) | collective-permute-done | bytes 524320 | tf_op jit(solution)/shard_map/ppermute | solution.py:59
  462.4 9.5 %collective-permute-done.74 = bf16[1,256,1024]{2,1,0:T(8,128)(2,1)S(1)} collective-permute-done((bf16[1,256,1024]{2,1,0:T(8,128)(2,1)S(1)}, bf16[1,256,1024]{2,1,0:T(8,128)(2,1)S(1)}, u32[]{:S(2)}, u32[]{:S(2)}) %collective-permute-start.74) | collective-permute-done | bytes 524320 | tf_op jit(solution)/shard_map/ppermute | solution.py:59
  473.4 10.3 %collective-permute-done.70 = bf16[2,128,1024]{2,1,0:T(8,128)(2,1)S(1)} collective-permute-done((bf16[2,128,1024]{2,1,0:T(8,128)(2,1)S(1)}, bf16[2,128,1024]{2,1,0:T(8,128)(2,1)S(1)}, u32[]{:S(2)}, u32[]{:S(2)}) %collective-permute-start.70) | collective-permute-done | bytes 524320 | tf_op jit(solution)/shard_map/ppermute | solution.py:59
  486.3 15.4 %collective-permute-done.77 = bf16[128,1024]{1,0:T(8,128)(2,1)S(1)} collective-permute-done((bf16[128,1024]{1,0:T(8,128)(2,1)S(1)}, bf16[128,1024]{1,0:T(8,128)(2,1)S(1)}, u32[]{:S(2)}, u32[]{:S(2)}) %collective-permute-start.77) | collective-permute-done | bytes 262176 | tf_op jit(solution)/shard_map/ppermute | solution.py:59
  503.6 3.0 collective-permute-start.79
  507.1 8.3 %collective-permute-done.79 = bf16[1,2,128,1024]{3,2,1,0:T(8,128)(2,1)S(1)} collective-permute-done((bf16[1,2,128,1024]{3,2,1,0:T(8,128)(2,1)S(1)}, bf16[1,2,128,1024]{3,2,1,0:T(8,128)(2,1)S(1)}, u32[]{:S(2)}, u32[]{:S(2)}) %collective-permute-start.79) | collective-permute-done | bytes 524320 | tf_op jit(solution)/shard_map/ppermute | solution.py:59
  519.3 8.3 %collective-permute-start.80 = (bf16[128,1024]{1,0:T(8,128)(2,1)S(1)}, bf16[128,1024]{1,0:T(8,128)(2,1)S(1)}, u32[]{:S(2)}, u32[]{:S(2)}) collective-permute-start(bf16[128,1024]{1,0:T(8,128)(2,1)S(1)} %dynamic-slice_bitcast_fusion.8), channel_id=1, source_target_pairs={{0,16},{4,20},{8,24},{12,28},{16,0},{20,4},{24,8},{28,12},{1,17},{... | collective-permute-start | bytes 786440 | tf_op jit(solution)/shard_map/ppermute | solution.py:59
  530.4 8.3 %collective-permute-done.82 = bf16[1,3,128,1024]{3,2,1,0:T(8,128)(2,1)S(1)} collective-permute-done((bf16[1,3,128,1024]{3,2,1,0:T(8,128)(2,1)S(1)}, bf16[1,3,128,1024]{3,2,1,0:T(8,128)(2,1)S(1)}, u32[]{:S(2)}, u32[]{:S(2)}) %collective-permute-start.82) | collective-permute-done | bytes 786464 | tf_op jit(solution)/shard_map/ppermute | solution.py:59
  540.4 8.4 %collective-permute-done.83 = bf16[1,1,128,1024]{3,2,1,0:T(8,128)(2,1)S(1)} collective-permute-done((bf16[1,1,128,1024]{3,2,1,0:T(8,128)(2,1)S(1)}, bf16[1,1,128,1024]{3,2,1,0:T(8,128)(2,1)S(1)}, u32[]{:S(2)}, u32[]{:S(2)}) %collective-permute-start.83) | collective-permute-done | bytes 262176 | tf_op jit(solution)/shard_map/ppermute | solution.py:59
  549.7 4.0 shard_map.301
  563.1 3.4 pad_maximum_fusion.1.in_ref
  566.5 4.8 shard_map.302
  (598 shorter events, 233.3 us)
Async XLA Ops:
  7.2 203.3 %all-gather.7.cloned.1.call-start = ((), (), s32[]{:S(2)}) async-start(), calls=%async_computation.2 | async-start | bytes 2359296 | tf_op jit(solution)/shard_map/all_gather | solution.py:501
  8.0 12.8 %collective-permute-start.1 = (bf16[1,4,128]{2,1,0:T(4,128)(2,1)S(1)}, bf16[1,4,128]{2,1,0:T(4,128)(2,1)S(1)}, u32[]{:S(2)}, u32[]{:S(2)}) collective-permute-start(bf16[1,4,128]{2,1,0:T(4,128)(2,1)S(1)} %maximum_bitcast_fusion.2), channel_id=1, source_target_pairs={{0,16},{4,20},{8,24},{12,28},{16,0},{20,4},{24,8},{28,12},{1,17},{... | collective-permute-start | bytes 3080 | tf_op jit(solution)/shard_map/ppermute | solution.py:59
  19.4 14.3 %collective-permute-start = (bf16[1,128,1024]{2,1,0:T(8,128)(2,1)}, bf16[1,128,1024]{2,1,0:T(8,128)(2,1)S(1)}, u32[]{:S(2)}, u32[]{:S(2)}) collective-permute-start(bf16[1,128,1024]{2,1,0:T(8,128)(2,1)} %get-tuple-element.143), channel_id=1, source_target_pairs={{0,16},{4,20},{8,24},{12,28},{16,0},{20,4},{24,8},{28,12},{1,17},{... | collective-permute-start | bytes 786440 | tf_op jit(solution)/shard_map/ppermute | solution.py:59
  36.1 13.8 %collective-permute-start.8 = (bf16[1,256,1024]{2,1,0:T(8,128)(2,1)S(1)}, bf16[1,256,1024]{2,1,0:T(8,128)(2,1)S(1)}, u32[]{:S(2)}, u32[]{:S(2)}) collective-permute-start(bf16[1,256,1024]{2,1,0:T(8,128)(2,1)S(1)} %fusion.75), channel_id=1, source_target_pairs={{0,2},{1,3},{2,0},{3,1},{4,6},{5,7},{6,4},{7,5},{8,10},{9,11},{10,... | collective-permute-start | bytes 1572872 | tf_op jit(solution)/shard_map/ppermute | solution.py:59
  36.7 13.1 %collective-permute-start.7 = (bf16[1,128,1024]{2,1,0:T(8,128)(2,1)S(1)}, bf16[1,128,1024]{2,1,0:T(8,128)(2,1)S(1)}, u32[]{:S(2)}, u32[]{:S(2)}) collective-permute-start(bf16[1,128,1024]{2,1,0:T(8,128)(2,1)S(1)} %copy-done.71), channel_id=1, source_target_pairs={{0,16},{4,20},{8,24},{12,28},{16,0},{20,4},{24,8},{28,12},{1,17},{... | collective-permute-start | bytes 786440 | tf_op jit(solution)/shard_map/ppermute | solution.py:59
  36.8 18.9 %collective-permute-start.6 = (bf16[2,128,1024]{2,1,0:T(8,128)(2,1)S(1)}, bf16[2,128,1024]{2,1,0:T(8,128)(2,1)S(1)}, u32[]{:S(2)}, u32[]{:S(2)}) collective-permute-start(bf16[2,128,1024]{2,1,0:T(8,128)(2,1)S(1)} %pad_maximum_fusion.11.refs_0_), channel_id=1, source_target_pairs={{0,8},{4,12},{8,0},{12,4},{16,24},{20,28},{24,16},{28,20},{1,9},{5... | collective-permute-start | bytes 1572872 | tf_op jit(solution)/shard_map/ppermute | solution.py:59
  56.5 32.4 %collective-permute-start.13 = (bf16[2,256,1024]{2,1,0:T(8,128)(2,1)S(1)}, bf16[2,256,1024]{2,1,0:T(8,128)(2,1)S(1)}, u32[]{:S(2)}, u32[]{:S(2)}) collective-permute-start(bf16[2,256,1024]{2,1,0:T(8,128)(2,1)S(1)} %pad_maximum_fusion.4), channel_id=1, source_target_pairs={{0,1},{1,0},{2,3},{3,2},{4,5},{5,4},{6,7},{7,6},{8,9},{9,8},{10,11... | collective-permute-start | bytes 3145736 | tf_op jit(solution)/shard_map/ppermute | solution.py:59
  58.7 209.1 %all-gather.9.cloned.1.call-start = ((), (), s32[]{:S(2)}) async-start(), calls=%async_computation.3 | async-start | bytes 2359296 | tf_op jit(solution)/shard_map/all_gather | solution.py:501
  58.9 17.9 %collective-permute-start.12 = (bf16[1,128,1024]{2,1,0:T(8,128)(2,1)S(1)}, bf16[1,128,1024]{2,1,0:T(8,128)(2,1)S(1)}, u32[]{:S(2)}, u32[]{:S(2)}) collective-permute-start(bf16[1,128,1024]{2,1,0:T(8,128)(2,1)S(1)} %copy-done.70), channel_id=1, source_target_pairs={{0,16},{4,20},{8,24},{12,28},{16,0},{20,4},{24,8},{28,12},{1,17},{... | collective-permute-start | bytes 786440 | tf_op jit(solution)/shard_map/ppermute | solution.py:59
  59.2 18.4 %collective-permute-start.9 = (bf16[2,128,1024]{2,1,0:T(8,128)(2,1)}, bf16[2,128,1024]{2,1,0:T(8,128)(2,1)S(1)}, u32[]{:S(2)}, u32[]{:S(2)}) collective-permute-start(bf16[2,128,1024]{2,1,0:T(8,128)(2,1)} %copy-done.32), channel_id=1, source_target_pairs={{0,4},{4,0},{8,12},{12,8},{16,20},{20,16},{24,28},{28,24},{1,5},{5... | collective-permute-start | bytes 1572872 | tf_op jit(solution)/shard_map/ppermute | solution.py:59
  60.8 26.8 %collective-permute-start.10 = (bf16[2,128,1024]{2,1,0:T(8,128)(2,1)}, bf16[2,128,1024]{2,1,0:T(8,128)(2,1)S(1)}, u32[]{:S(2)}, u32[]{:S(2)}) collective-permute-start(bf16[2,128,1024]{2,1,0:T(8,128)(2,1)} %copy-done.62), channel_id=1, source_target_pairs={{0,4},{4,0},{8,12},{12,8},{16,20},{20,16},{24,28},{28,24},{1,5},{5... | collective-permute-start | bytes 1572872 | tf_op jit(solution)/shard_map/ppermute | solution.py:59
  61.3 27.6 %collective-permute-start.11 = (bf16[2,128,1024]{2,1,0:T(8,128)(2,1)S(1)}, bf16[2,128,1024]{2,1,0:T(8,128)(2,1)S(1)}, u32[]{:S(2)}, u32[]{:S(2)}) collective-permute-start(bf16[2,128,1024]{2,1,0:T(8,128)(2,1)S(1)} %pad_maximum_fusion.12.refs_0_), channel_id=1, source_target_pairs={{0,8},{4,12},{8,0},{12,4},{16,24},{20,28},{24,16},{28,20},{1,9},{5... | collective-permute-start | bytes 1572872 | tf_op jit(solution)/shard_map/ppermute | solution.py:59
  106.2 14.9 %collective-permute-start.14 = (bf16[2,128,1024]{2,1,0:T(8,128)(2,1)S(1)}, bf16[2,128,1024]{2,1,0:T(8,128)(2,1)}, u32[]{:S(2)}, u32[]{:S(2)}) collective-permute-start(bf16[2,128,1024]{2,1,0:T(8,128)(2,1)S(1)} %copy-done.31), channel_id=1, source_target_pairs={{0,4},{4,0},{8,12},{12,8},{16,20},{20,16},{24,28},{28,24},{1,5},{5... | collective-permute-start | bytes 1572872 | tf_op jit(solution)/shard_map/ppermute | solution.py:59
  107.7 24.1 %collective-permute-start.15 = (bf16[2,128,1024]{2,1,0:T(8,128)(2,1)S(1)}, bf16[2,128,1024]{2,1,0:T(8,128)(2,1)}, u32[]{:S(2)}, u32[]{:S(2)}) collective-permute-start(bf16[2,128,1024]{2,1,0:T(8,128)(2,1)S(1)} %copy-done.61), channel_id=1, source_target_pairs={{0,4},{4,0},{8,12},{12,8},{16,20},{20,16},{24,28},{28,24},{1,5},{5... | collective-permute-start | bytes 1572872 | tf_op jit(solution)/shard_map/ppermute | solution.py:59
  108.2 23.7 %collective-permute-start.16 = (bf16[2,128,1024]{2,1,0:T(8,128)(2,1)}, bf16[2,128,1024]{2,1,0:T(8,128)(2,1)}, u32[]{:S(2)}, u32[]{:S(2)}) collective-permute-start(bf16[2,128,1024]{2,1,0:T(8,128)(2,1)} %pad_maximum_fusion.13.refs_0_), channel_id=1, source_target_pairs={{0,8},{4,12},{8,0},{12,4},{16,24},{20,28},{24,16},{28,20},{1,9},{5... | collective-permute-start | bytes 1572872 | tf_op jit(solution)/shard_map/ppermute | solution.py:59
  131.9 13.5 %collective-permute-start.21 = (bf16[1,256,1024]{2,1,0:T(8,128)(2,1)S(1)}, bf16[1,256,1024]{2,1,0:T(8,128)(2,1)S(1)}, u32[]{:S(2)}, u32[]{:S(2)}) collective-permute-start(bf16[1,256,1024]{2,1,0:T(8,128)(2,1)S(1)} %slice.421), channel_id=1, source_target_pairs={{0,2},{1,3},{2,0},{3,1},{4,6},{5,7},{6,4},{7,5},{8,10},{9,11},{10,... | collective-permute-start | bytes 1572872 | tf_op jit(solution)/shard_map/ppermute | solution.py:59
  133.5 137.3 %all-gather.11.cloned.1.call-start = ((), (), s32[]{:S(2)}) async-start(), calls=%async_computation.4 | async-start | bytes 2359296 | tf_op jit(solution)/shard_map/all_gather | solution.py:501
  147.9 12.8 %collective-permute-start.24 = (bf16[1,256,1024]{2,1,0:T(8,128)(2,1)S(1)}, bf16[1,256,1024]{2,1,0:T(8,128)(2,1)S(1)}, u32[]{:S(2)}, u32[]{:S(2)}) collective-permute-start(bf16[1,256,1024]{2,1,0:T(8,128)(2,1)S(1)} %fusion.78), channel_id=1, source_target_pairs={{0,2},{1,3},{2,0},{3,1},{4,6},{5,7},{6,4},{7,5},{8,10},{9,11},{10,... | collective-permute-start | bytes 1572872 | tf_op jit(solution)/shard_map/ppermute | solution.py:59
  160.8 23.4 %collective-permute-start.22 = (bf16[2,128,1024]{2,1,0:T(8,128)(2,1)}, bf16[2,128,1024]{2,1,0:T(8,128)(2,1)}, u32[]{:S(2)}, u32[]{:S(2)}) collective-permute-start(bf16[2,128,1024]{2,1,0:T(8,128)(2,1)} %pad_maximum_fusion.13.refs_0_), channel_id=1, source_target_pairs={{0,4},{4,0},{8,12},{12,8},{16,20},{20,16},{24,28},{28,24},{1,5},{5... | collective-permute-start | bytes 1572872 | tf_op jit(solution)/shard_map/ppermute | solution.py:59
  162.4 33.0 %collective-permute-start.23 = (bf16[2,128,1024]{2,1,0:T(8,128)(2,1)}, bf16[2,128,1024]{2,1,0:T(8,128)(2,1)}, u32[]{:S(2)}, u32[]{:S(2)}) collective-permute-start(bf16[2,128,1024]{2,1,0:T(8,128)(2,1)} %collective-permute-done.16.refs_1_), channel_id=1, source_target_pairs={{0,4},{4,0},{8,12},{12,8},{16,20},{20,16},{24,28},{28,24},{1,5},{5... | collective-permute-start | bytes 1572872 | tf_op jit(solution)/shard_map/ppermute | solution.py:59
  202.1 315.4 %reduce-scatter.2.cloned.1.call-start = ((), (), s32[]{:S(2)}) async-start(), calls=%async_computation.1 | async-start | bytes 4718592 | tf_op jit(solution)/shard_map/reduce_scatter | solution.py:593
  208.0 15.0 %collective-permute-start.27 = (bf16[1,256,1024]{2,1,0:T(8,128)(2,1)}, bf16[1,256,1024]{2,1,0:T(8,128)(2,1)S(1)}, u32[]{:S(2)}, u32[]{:S(2)}) collective-permute-start(bf16[1,256,1024]{2,1,0:T(8,128)(2,1)} %fusion.91), channel_id=1, source_target_pairs={{0,2},{1,3},{2,0},{3,1},{4,6},{5,7},{6,4},{7,5},{8,10},{9,11},{10,... | collective-permute-start | bytes 1572872 | tf_op jit(solution)/shard_map/ppermute | solution.py:59
  212.5 16.3 %collective-permute-start.30 = (bf16[256,256]{1,0:T(8,128)(2,1)}, bf16[256,256]{1,0:T(8,128)(2,1)}, u32[]{:S(2)}, u32[]{:S(2)}) collective-permute-start(bf16[256,256]{1,0:T(8,128)(2,1)} %get-tuple-element.307), channel_id=1, source_target_pairs={{0,2},{1,3},{2,0},{3,1},{4,6},{5,7},{6,4},{7,5},{8,10},{9,11},{10,... | collective-permute-start | bytes 393224 | tf_op jit(solution)/shard_map/ppermute | solution.py:59
  213.1 15.8 %collective-permute-start.32 = (bf16[256,256]{1,0:T(8,128)(2,1)}, bf16[256,256]{1,0:T(8,128)(2,1)}, u32[]{:S(2)}, u32[]{:S(2)}) collective-permute-start(bf16[256,256]{1,0:T(8,128)(2,1)} %get-tuple-element.308), channel_id=1, source_target_pairs={{0,1},{1,0},{2,3},{3,2},{4,5},{5,4},{6,7},{7,6},{8,9},{9,8},{10,11... | collective-permute-start | bytes 393224 | tf_op jit(solution)/shard_map/ppermute | solution.py:59
  213.1 15.8 %collective-permute-start.31 = (bf16[256,256]{1,0:T(8,128)(2,1)S(1)}, bf16[256,256]{1,0:T(8,128)(2,1)}, u32[]{:S(2)}, u32[]{:S(2)}) collective-permute-start(bf16[256,256]{1,0:T(8,128)(2,1)S(1)} %get-tuple-element.310), channel_id=1, source_target_pairs={{0,3},{1,2},{2,1},{3,0},{4,7},{5,6},{6,5},{7,4},{8,11},{9,10},{10,... | collective-permute-start | bytes 393224 | tf_op jit(solution)/shard_map/ppermute | solution.py:59
  240.2 19.0 %collective-permute-start.39 = (bf16[1,256,1024]{2,1,0:T(8,128)(2,1)}, bf16[1,256,1024]{2,1,0:T(8,128)(2,1)}, u32[]{:S(2)}, u32[]{:S(2)}) collective-permute-start(bf16[1,256,1024]{2,1,0:T(8,128)(2,1)} %param.21), channel_id=1, source_target_pairs={{0,2},{1,3},{2,0},{3,1},{4,6},{5,7},{6,4},{7,5},{8,10},{9,11},{10,... | collective-permute-start | bytes 1572872 | tf_op jit(solution)/shard_map/ppermute | solution.py:59
  261.1 20.2 %collective-permute-start.40 = (bf16[2,256,1024]{2,1,0:T(8,128)(2,1)}, bf16[2,256,1024]{2,1,0:T(8,128)(2,1)}, u32[]{:S(2)}, u32[]{:S(2)}) collective-permute-start(bf16[2,256,1024]{2,1,0:T(8,128)(2,1)} %constant_dynamic-update-slice_fusion), channel_id=1, source_target_pairs={{0,1},{1,0},{2,3},{3,2},{4,5},{5,4},{6,7},{7,6},{8,9},{9,8},{10,11... | collective-permute-start | bytes 3145736 | tf_op jit(solution)/shard_map/ppermute | solution.py:59
  306.8 12.7 %collective-permute-start.47 = (bf16[256,256]{1,0:T(8,128)(2,1)S(1)}, bf16[256,256]{1,0:T(8,128)(2,1)S(1)}, u32[]{:S(2)}, u32[]{:S(2)}) collective-permute-start(bf16[256,256]{1,0:T(8,128)(2,1)S(1)} %get-tuple-element.299), channel_id=1, source_target_pairs={{0,2},{1,3},{2,0},{3,1},{4,6},{5,7},{6,4},{7,5},{8,10},{9,11},{10,... | collective-permute-start | bytes 393224 | tf_op jit(solution)/shard_map/ppermute | solution.py:59
  308.3 13.8 %collective-permute-start.48 = (bf16[256,256]{1,0:T(8,128)(2,1)S(1)}, bf16[256,256]{1,0:T(8,128)(2,1)S(1)}, u32[]{:S(2)}, u32[]{:S(2)}) collective-permute-start(bf16[256,256]{1,0:T(8,128)(2,1)S(1)} %get-tuple-element.302), channel_id=1, source_target_pairs={{0,3},{1,2},{2,1},{3,0},{4,7},{5,6},{6,5},{7,4},{8,11},{9,10},{10,... | collective-permute-start | bytes 393224 | tf_op jit(solution)/shard_map/ppermute | solution.py:59
  330.2 14.9 %collective-permute-start.57 = (f32[1024]{0:T(1024)S(1)}, f32[1024]{0:T(1024)S(1)}, u32[]{:S(2)}, u32[]{:S(2)}) collective-permute-start(f32[1024]{0:T(1024)S(1)} %add.448), channel_id=1, source_target_pairs={{0,1},{1,0},{2,3},{3,2},{4,5},{5,4},{6,7},{7,6},{8,9},{9,8},{10,11... | collective-permute-start | bytes 12296 | tf_op jit(solution)/shard_map/ppermute | solution.py:59
  330.7 25.5 %collective-permute-start.55 = (bf16[2,2,128,1024]{3,2,0,1:T(8,128)(2,1)S(1)}, bf16[2,2,128,1024]{3,2,0,1:T(8,128)(2,1)S(1)}, u32[]{:S(2)}, u32[]{:S(2)}) collective-permute-start(bf16[2,2,128,1024]{3,2,0,1:T(8,128)(2,1)S(1)} %pad_maximum_fusion.6), channel_id=1, source_target_pairs={{0,4},{4,0},{8,12},{12,8},{16,20},{20,16},{24,28},{28,24},{1,5},{5... | collective-permute-start | bytes 3145736 | tf_op jit(solution)/shard_map/ppermute | solution.py:59
  356.2 24.9 %collective-permute-start.62 = (f32[1024]{0:T(1024)S(1)}, f32[1024]{0:T(1024)S(1)}, u32[]{:S(2)}, u32[]{:S(2)}) collective-permute-start(f32[1024]{0:T(1024)S(1)} %add.461), channel_id=1, source_target_pairs={{0,16},{4,20},{8,24},{12,28},{16,0},{20,4},{24,8},{28,12},{1,17},{... | collective-permute-start | bytes 12296 | tf_op jit(solution)/shard_map/ppermute | solution.py:59
  358.8 13.1 %collective-permute-start.60 = (bf16[1,256,1024]{2,1,0:T(8,128)(2,1)S(1)}, bf16[1,256,1024]{2,1,0:T(8,128)(2,1)S(1)}, u32[]{:S(2)}, u32[]{:S(2)}) collective-permute-start(bf16[1,256,1024]{2,1,0:T(8,128)(2,1)S(1)} %slice.420), channel_id=1, source_target_pairs={{0,2},{1,3},{2,0},{3,1},{4,6},{5,7},{6,4},{7,5},{8,10},{9,11},{10,... | collective-permute-start | bytes 1572872 | tf_op jit(solution)/shard_map/ppermute | solution.py:59
  360.0 27.4 %collective-permute-start.58 = (bf16[2,128,1024]{2,1,0:T(8,128)(2,1)S(1)}, bf16[2,128,1024]{2,1,0:T(8,128)(2,1)S(1)}, u32[]{:S(2)}, u32[]{:S(2)}) collective-permute-start(bf16[2,128,1024]{2,1,0:T(8,128)(2,1)S(1)} %dynamic-slice_bitcast_fusion.7), channel_id=1, source_target_pairs={{0,8},{4,12},{8,0},{12,4},{16,24},{20,28},{24,16},{28,20},{1,9},{5... | collective-permute-start | bytes 1572872 | tf_op jit(solution)/shard_map/ppermute | solution.py:59
  361.6 25.8 %collective-permute-start.59 = (bf16[2,2,128,1024]{3,2,0,1:T(8,128)(2,1)S(1)}, bf16[2,2,128,1024]{3,2,0,1:T(8,128)(2,1)S(1)}, u32[]{:S(2)}, u32[]{:S(2)}) collective-permute-start(bf16[2,2,128,1024]{3,2,0,1:T(8,128)(2,1)S(1)} %copy_bitcast_fusion.1), channel_id=1, source_target_pairs={{0,4},{4,0},{8,12},{12,8},{16,20},{20,16},{24,28},{28,24},{1,5},{5... | collective-permute-start | bytes 3145736 | tf_op jit(solution)/shard_map/ppermute | solution.py:59
  388.6 30.6 %collective-permute-start.68 = (f32[1024]{0:T(1024)S(1)}, f32[1024]{0:T(1024)S(1)}, u32[]{:S(2)}, u32[]{:S(2)}) collective-permute-start(f32[1024]{0:T(1024)S(1)} %add.468), channel_id=1, source_target_pairs={{0,8},{4,12},{8,0},{12,4},{16,24},{20,28},{24,16},{28,20},{1,9},{5... | collective-permute-start | bytes 12296 | tf_op jit(solution)/shard_map/ppermute | solution.py:59
  404.5 14.8 %collective-permute-start.67 = (bf16[512,1024]{1,0:T(8,128)(2,1)}, bf16[512,1024]{1,0:T(8,128)(2,1)}, u32[]{:S(2)}, u32[]{:S(2)}) collective-permute-start(bf16[512,1024]{1,0:T(8,128)(2,1)} %convolution_convert_fusion.4), channel_id=1, source_target_pairs={{0,1},{1,0},{2,3},{3,2},{4,5},{5,4},{6,7},{7,6},{8,9},{9,8},{10,11... | collective-permute-start | bytes 3145736 | tf_op jit(solution)/shard_map/ppermute | solution.py:59
  412.2 27.1 %collective-permute-start.63 = (bf16[128,1024]{1,0:T(8,128)(2,1)S(1)}, bf16[128,1024]{1,0:T(8,128)(2,1)S(1)}, u32[]{:S(2)}, u32[]{:S(2)}) collective-permute-start(bf16[128,1024]{1,0:T(8,128)(2,1)S(1)} %dynamic-slice_bitcast_fusion.13), channel_id=1, source_target_pairs={{0,16},{4,20},{8,24},{12,28},{16,0},{20,4},{24,8},{28,12},{1,17},{... | collective-permute-start | bytes 786440 | tf_op jit(solution)/shard_map/ppermute | solution.py:59
  414.3 32.0 %collective-permute-start.65 = (bf16[2,2,128,1024]{3,2,0,1:T(8,128)(2,1)S(1)}, bf16[2,2,128,1024]{3,2,0,1:T(8,128)(2,1)S(1)}, u32[]{:S(2)}, u32[]{:S(2)}) collective-permute-start(bf16[2,2,128,1024]{3,2,0,1:T(8,128)(2,1)S(1)} %copy_bitcast_fusion), channel_id=1, source_target_pairs={{0,4},{4,0},{8,12},{12,8},{16,20},{20,16},{24,28},{28,24},{1,5},{5... | collective-permute-start | bytes 3145736 | tf_op jit(solution)/shard_map/ppermute | solution.py:59
  416.7 29.5 %collective-permute-start.64 = (bf16[2,128,1024]{2,1,0:T(8,128)(2,1)S(1)}, bf16[2,128,1024]{2,1,0:T(8,128)(2,1)S(1)}, u32[]{:S(2)}, u32[]{:S(2)}) collective-permute-start(bf16[2,128,1024]{2,1,0:T(8,128)(2,1)S(1)} %dynamic-slice_bitcast_fusion.6), channel_id=1, source_target_pairs={{0,8},{4,12},{8,0},{12,4},{16,24},{20,28},{24,16},{28,20},{1,9},{5... | collective-permute-start | bytes 1572872 | tf_op jit(solution)/shard_map/ppermute | solution.py:59
  448.2 25.2 %collective-permute-start.69 = (bf16[128,1024]{1,0:T(8,128)(2,1)S(1)}, bf16[128,1024]{1,0:T(8,128)(2,1)S(1)}, u32[]{:S(2)}, u32[]{:S(2)}) collective-permute-start(bf16[128,1024]{1,0:T(8,128)(2,1)S(1)} %dynamic-slice_bitcast_fusion.12), channel_id=1, source_target_pairs={{0,16},{4,20},{8,24},{12,28},{16,0},{20,4},{24,8},{28,12},{1,17},{... | collective-permute-start | bytes 786440 | tf_op jit(solution)/shard_map/ppermute | solution.py:59
  458.0 13.9 %collective-permute-start.74 = (bf16[1,256,1024]{2,1,0:T(8,128)(2,1)S(1)}, bf16[1,256,1024]{2,1,0:T(8,128)(2,1)S(1)}, u32[]{:S(2)}, u32[]{:S(2)}) collective-permute-start(bf16[1,256,1024]{2,1,0:T(8,128)(2,1)S(1)} %slice.419), channel_id=1, source_target_pairs={{0,2},{1,3},{2,0},{3,1},{4,6},{5,7},{6,4},{7,5},{8,10},{9,11},{10,... | collective-permute-start | bytes 1572872 | tf_op jit(solution)/shard_map/ppermute | solution.py:59
  460.1 23.5 %collective-permute-start.70 = (bf16[2,128,1024]{2,1,0:T(8,128)(2,1)S(1)}, bf16[2,128,1024]{2,1,0:T(8,128)(2,1)S(1)}, u32[]{:S(2)}, u32[]{:S(2)}) collective-permute-start(bf16[2,128,1024]{2,1,0:T(8,128)(2,1)S(1)} %dynamic-slice_bitcast_fusion.5), channel_id=1, source_target_pairs={{0,8},{4,12},{8,0},{12,4},{16,24},{20,28},{24,16},{28,20},{1,9},{5... | collective-permute-start | bytes 1572872 | tf_op jit(solution)/shard_map/ppermute | solution.py:59
  483.9 19.4 %collective-permute-start.76 = (bf16[2,2,128,1024]{3,2,0,1:T(8,128)(2,1)S(1)}, bf16[2,2,128,1024]{3,2,0,1:T(8,128)(2,1)S(1)}, u32[]{:S(2)}, u32[]{:S(2)}) collective-permute-start(bf16[2,2,128,1024]{3,2,0,1:T(8,128)(2,1)S(1)} %pad_maximum_fusion.8), channel_id=1, source_target_pairs={{0,4},{4,0},{8,12},{12,8},{16,20},{20,16},{24,28},{28,24},{1,5},{5... | collective-permute-start | bytes 3145736 | tf_op jit(solution)/shard_map/ppermute | solution.py:59
  484.2 17.4 %collective-permute-start.77 = (bf16[128,1024]{1,0:T(8,128)(2,1)S(1)}, bf16[128,1024]{1,0:T(8,128)(2,1)S(1)}, u32[]{:S(2)}, u32[]{:S(2)}) collective-permute-start(bf16[128,1024]{1,0:T(8,128)(2,1)S(1)} %dynamic-slice_bitcast_fusion.10), channel_id=1, source_target_pairs={{0,16},{4,20},{8,24},{12,28},{16,0},{20,4},{24,8},{28,12},{1,17},{... | collective-permute-start | bytes 786440 | tf_op jit(solution)/shard_map/ppermute | solution.py:59
  518.7 20.0 %collective-permute-start.82 = (bf16[1,3,128,1024]{3,2,1,0:T(8,128)(2,1)S(1)}, bf16[1,3,128,1024]{3,2,1,0:T(8,128)(2,1)S(1)}, u32[]{:S(2)}, u32[]{:S(2)}) collective-permute-start(bf16[1,3,128,1024]{3,2,1,0:T(8,128)(2,1)S(1)} %maximum_bitcast_fusion), channel_id=1, source_target_pairs={{0,2},{1,3},{2,0},{3,1},{4,6},{5,7},{6,4},{7,5},{8,10},{9,11},{10,... | collective-permute-start | bytes 2359304 | tf_op jit(solution)/shard_map/ppermute | solution.py:59
  519.3 20.6 %collective-permute-start.80 = (bf16[128,1024]{1,0:T(8,128)(2,1)S(1)}, bf16[128,1024]{1,0:T(8,128)(2,1)S(1)}, u32[]{:S(2)}, u32[]{:S(2)}) collective-permute-start(bf16[128,1024]{1,0:T(8,128)(2,1)S(1)} %dynamic-slice_bitcast_fusion.8), channel_id=1, source_target_pairs={{0,16},{4,20},{8,24},{12,28},{16,0},{20,4},{24,8},{28,12},{1,17},{... | collective-permute-start | bytes 786440 | tf_op jit(solution)/shard_map/ppermute | solution.py:59
  540.0 23.1 %collective-permute-start.85 = (bf16[2,3,128,1024]{3,2,1,0:T(8,128)(2,1)S(1)}, bf16[2,3,128,1024]{3,2,1,0:T(8,128)(2,1)}, u32[]{:S(2)}, u32[]{:S(2)}) collective-permute-start(bf16[2,3,128,1024]{3,2,1,0:T(8,128)(2,1)S(1)} %pad_maximum_fusion.3), channel_id=1, source_target_pairs={{0,1},{1,0},{2,3},{3,2},{4,5},{5,4},{6,7},{7,6},{8,9},{9,8},{10,11... | collective-permute-start | bytes 4718600 | tf_op jit(solution)/shard_map/ppermute | solution.py:59
  (158 other events, 1171.5 us)
Sparse Core Ops, SparseCore 0:
  58.8 57.4 all-gather.6
  133.7 56.9 all-gather.8
  202.3 49.2 all-gather.10
  388.8 110.8 reduce-scatter.1
where the time goes:
time: 592 us; the launch traced here: 581 us
  waiting for transfers between devices  256 us (43%)
  starting transfers between devices  88.2 us (15%)
  matrix products  73.9 us (12%)
  other arithmetic  56.7 us (10%)
  Pallas kernels  54.2 us (9%)
  local copies, waits for them, and re-layouts  35.7 us (6%)
  between operations  16.4 us (3%)
    ppermute x86, waiting for transfers between devices, swap(): lax.ppermute(array, axis, [(i, i ^ bit) for i in range(self.sizes[axis])])  256 us
    ppermute x86, starting transfers between devices, swap(): lax.ppermute(array, axis, [(i, i ^ bit) for i in range(self.sizes[axis])])  87.8 us
    dot_general x12, matrix products, dot_rows(): return jnp.dot(left, right, preferred_element_type=F32)  31.1 us
    dot_general x12, matrix products, dot_back(): lax.dot_general(left, right, (((1,), (1,)), ((), ())), preferred_element_...  22.9 us
    pallas_call x3, Pallas kernels, attend_call(): pl.pallas_call(functools.partial(attend_back_kernel, heads), grid=(groups...  17.9 us
    dot_general x12, matrix products, dot_cross(): lax.dot_general(left, right, (((0,), (0,)), ((), ())), preferred_element_...  14.6 us
    unnamed x234, local copies, waits for them, and re-layouts  14.2 us
  transfers between devices with their start and end apart: 90, of which 42 were waited for; matrix products, arithmetic and copies ran while one was open for 24% of the time, Pallas kernels for 8%

commit v1 on v0

v1 whole, which is shorter than its diff:
```python
import functools

import jax
import jax.numpy as jnp
from jax import lax
from jax.experimental import pallas as pl
from jax.experimental.pallas import tpu as pltpu
from jax.sharding import PartitionSpec as P

HEADS = 16
EPS = 1e-06
NEG = -1e30
HIGH = lax.Precision.HIGHEST
LOW = jnp.bfloat16
F32 = jnp.float32
I32 = jnp.int32
VMEM_SPEC = pl.BlockSpec(memory_space=pltpu.VMEM)
SMEM_SPEC = pl.BlockSpec(memory_space=pltpu.SMEM)
ANY_SPEC = pl.BlockSpec(memory_space=pl.ANY)


def dot_rows(left, right):
    return jnp.dot(left, right, preferred_element_type=F32)


def dot_cross(left, right):
    return lax.dot_general(left, right, (((0,), (0,)), ((), ())), preferred_element_type=F32)


def dot_back(left, right):
    return lax.dot_general(left, right, (((1,), (1,)), ((), ())), preferred_element_type=F32)


def bits_of(size):
    found = []
    bit = size // 2
    while bit >= 1:
        found.append(bit)
        bit //= 2
    return found


def xor_blocks(array, index, blocks, axis):
    size = array.shape[axis] // blocks
    for bit in bits_of(blocks):
        parts = [
            lax.slice_in_dim(array, k * size, (k + 1) * size, axis=axis) for k in range(blocks)
        ]
        swapped = jnp.concatenate([parts[k ^ bit] for k in range(blocks)], axis=axis)
        array = jnp.where((index & bit) != 0, swapped, array)
    return array


class Links:
    def __init__(self, sizes):
        self.sizes = sizes

    def swap(self, array, axis, bit):
        return lax.ppermute(array, axis, [(i, i ^ bit) for i in range(self.sizes[axis])])

    def gather(self, local, axis, order):
        for bit in order:
            local = jnp.concatenate([local, self.swap(local, axis, bit)], 0)
        return local


class Gather:
    def __init__(self, links, piece, order):
        self.links = links
        self.arrays = [piece]
        self.offsets = [[0]]
        self.todo = [(order[0], None)]
        made = 1
        for bit in order[1:]:
            self.todo += [(bit, i) for i in range(made)]
            made *= 2

    def next(self, count=1):
        for bit, at in self.todo[:count]:
            got = self.links.swap(self.arrays[at or 0], "wide", bit)
            offsets = [k ^ bit for k in self.offsets[at or 0]]
            if at is None:
                self.arrays = [jnp.concatenate([self.arrays[0], got], 0)]
                self.offsets = [self.offsets[0] + offsets]
            else:
                self.arrays.append(got)
                self.offsets.append(offsets)
        self.todo = self.todo[count:]

    def finish(self):
        self.next(len(self.todo))
        return list(zip(self.offsets, self.arrays))


class Scatter:
    def __init__(self, links, columns, index, order):
        self.links = links
        self.index = index
        self.bits = bits_of(links.sizes["wide"])
        self.left = list(order[::-1])
        lead = (2,) * len(self.bits)
        size = links.sizes["wide"]
        self.base = [c.reshape(lead + (c.shape[0] // size, c.shape[1])) for c in columns]
        self.got = None
        self.at = None
        self.mine = None

    @property
    def arrays(self):
        return [self.base] if self.got is None else [self.base, self.got]

    @arrays.setter
    def arrays(self, values):
        self.base = values[0]
        if self.got is not None:
            self.got = values[1]

    def value(self):
        def pick(c):
            return lax.dynamic_index_in_dim(c, self.mine, self.at, keepdims=False)

        if self.got is None:
            return jnp.concatenate(self.base, -1) if len(self.base) > 1 else self.base[0]
        kept = jnp.concatenate([pick(c) for c in self.base], -1)
        return (kept.astype(F32) + self.got.astype(F32)).astype(LOW)

    def next(self):
        if not self.left:
            return
        bit = self.left.pop(0)
        at = self.bits.index(bit)
        mine = jnp.where((self.index & bit) != 0, 1, 0).astype(I32)
        if self.got is not None:
            self.base = [self.value()]
        send = jnp.concatenate(
            [lax.dynamic_index_in_dim(c, 1 - mine, at, keepdims=False) for c in self.base], -1
        )
        self.bits.pop(at)
        self.at, self.mine = at, mine
        self.got = self.links.swap(send, "wide", bit)

    def finish(self):
        while self.left:
            self.next()
        return self.value()


def sync(movers, *values):
    held = lax.optimization_barrier(([m.arrays for m in movers], values))
    for mover, arrays in zip(movers, held[0]):
        mover.arrays = arrays
    return held[1]


def order_of(order):
    offsets = [0]
    for bit in order:
        offsets = offsets + [k ^ bit for k in offsets]
    return offsets


def pack(index, narrow, shards, layouts):
    def kernel(index_ref, *refs):
        ins, outs, sems = refs[: len(shards)], refs[len(shards) : -1], refs[-1]
        at = index_ref[0]
        copies = []

        def add(source, target):
            copies.append(pltpu.make_async_copy(source, target, sems.at[len(copies)]))

        for (out, members), out_ref in zip(layouts, outs):
            low = 0
            for member, blocks, width in members:
                source = ins[member]
                if blocks is None:
                    size = source.shape[0] // narrow
                    row = pl.multiple_of(at * size, size)
                    cols = source.shape[1]
                    add(source.at[pl.ds(row, size), :], out_ref.at[0, :, low : low + cols])
                    low += cols
                    continue
                for block in range(blocks):
                    start = pl.multiple_of((block * narrow + at) * width, width)
                    add(source.at[:, pl.ds(start, width)], out_ref.at[0, :, low : low + width])
                    low += width
        for copy in copies:
            copy.start()
        for copy in copies:
            copy.wait()

    count = sum(1 if m[1] is None else m[1] for _, members in layouts for m in members)
    return pl.pallas_call(
        kernel,
        out_shape=[jax.ShapeDtypeStruct((1,) + shape, LOW) for shape, _ in layouts],
        in_specs=[SMEM_SPEC] + [ANY_SPEC] * len(shards),
        out_specs=[VMEM_SPEC] * len(layouts),
        scratch_shapes=[pltpu.SemaphoreType.DMA((count,))],
    )(index.reshape(1), *shards)


def assemble(sources, index, widths):
    own = sources[0][0][0][1].shape[1]
    arrays = [array for parts, _ in sources for _, array in parts]
    rows = sum(len(ks) for ks, _ in sources[0][0]) * own
    count = sum(len(ks) * len(spans) for parts, spans in sources for ks, _ in parts)

    def kernel(index_ref, *refs):
        ins, outs, sems = refs[: len(arrays)], refs[len(arrays) : -1], refs[-1]
        copies = []
        at_ref = 0
        for parts, spans in sources:
            for ks, _ in parts:
                for j, k in enumerate(ks):
                    row = pl.multiple_of((index_ref[0] ^ k) * own, own)
                    for low, high, out, at in spans:
                        copies.append(
                            pltpu.make_async_copy(
                                ins[at_ref].at[j, :, low:high],
                                outs[out].at[pl.ds(row, own), at : at + high - low],
                                sems.at[len(copies)],
                            )
                        )
                at_ref += 1
        for copy in copies:
            copy.start()
        for copy in copies:
            copy.wait()

    return pl.pallas_call(
        kernel,
        out_shape=[jax.ShapeDtypeStruct((rows, width), LOW) for width in widths],
        in_specs=[SMEM_SPEC] + [ANY_SPEC] * len(arrays),
        out_specs=[VMEM_SPEC] * len(widths),
        scratch_shapes=[pltpu.SemaphoreType.DMA((count,))],
    )(index.reshape(1), *arrays)


def head_columns(ref, part, head, heads, width):
    start = (part * heads + head) * width
    return ref[:, start : start + width]


def head_prob(query, key, bias):
    scores = dot_back(query, key) + bias
    lifted = jnp.exp(scores - jnp.max(scores, -1, keepdims=True))
    return lifted / jnp.sum(lifted, -1, keepdims=True)


def write_part(part_refs, value):
    for i, ref in enumerate(part_refs):

        @pl.when(pl.program_id(0) == i)
        def _():
            ref[...] = value


def attend_kernel(
    heads, normed_ref, qkv_ref, proj_ref, bias_ref, combined_ref, out_ref, *part_refs
):
    width = out_ref.shape[1] // heads
    bias = bias_ref[0]
    combined_ref[...] = dot_rows(normed_ref[...], qkv_ref[...]).astype(LOW)
    outs = []
    for head in range(heads):
        query = head_columns(combined_ref, 0, head, heads, width) * LOW(width**-0.5)
        key = head_columns(combined_ref, 1, head, heads, width)
        val = head_columns(combined_ref, 2, head, heads, width)
        prob = head_prob(query, key, bias).astype(LOW)
        outs.append(dot_rows(prob, val).astype(LOW))
    attended = jnp.concatenate(outs, 1)
    out_ref[...] = attended
    write_part(part_refs, dot_rows(attended, proj_ref[...]).astype(LOW))


def attend_back_kernel(
    heads, grad_ref, qkv_ref, proj_ref, bias_ref, combined_ref, out_ref, *rest
):
    part_refs, low_ref = rest[:-1], rest[-1]
    width = low_ref.shape[1] // heads
    scale = width**-0.5
    bias = bias_ref[0]
    low_ref[...] = dot_back(grad_ref[...], proj_ref[...]).astype(LOW)
    outs = [[], [], []]
    for head in range(heads):
        query = head_columns(combined_ref, 0, head, heads, width) * LOW(scale)
        key = head_columns(combined_ref, 1, head, heads, width)
        val = head_columns(combined_ref, 2, head, heads, width)
        grad = head_columns(low_ref, 0, head, heads, width)
        prob = head_prob(query, key, bias)
        prob_grad = dot_back(grad, val)
        inner = jnp.sum(prob * prob_grad, -1, keepdims=True)
        score_grad = (prob * (prob_grad - inner)).astype(LOW)
        outs[0].append((dot_rows(score_grad, key) * scale).astype(LOW))
        outs[1].append(dot_cross(score_grad, query).astype(LOW))
        outs[2].append(dot_cross(prob.astype(LOW), grad).astype(LOW))
    combined_grad = jnp.concatenate(outs[0] + outs[1] + outs[2], 1)
    out_ref[...] = combined_grad
    write_part(part_refs, dot_back(combined_grad, qkv_ref[...]).astype(LOW))


def attend_call(heads, values, qkv, proj, bias, combined=None):
    groups, rows, _ = bias.shape
    width = values.shape[1]
    third = proj.shape[0]
    total = groups * rows

    def rows_spec(cols):
        return pl.BlockSpec((rows, cols), lambda i: (i, 0))

    def whole_spec(array):
        return pl.BlockSpec(array.shape, lambda i: (0, 0))

    bias_spec = pl.BlockSpec((1, rows, rows), lambda i: (i, 0, 0))
    in_specs = [rows_spec(width), whole_spec(qkv), whole_spec(proj), bias_spec]
    wide_out = jax.ShapeDtypeStruct((total, 3 * third), LOW)
    part_outs = [jax.ShapeDtypeStruct((rows, width), LOW)] * groups
    part_specs = [pl.BlockSpec((rows, width), lambda i: (0, 0))] * groups
    if combined is None:
        return pl.pallas_call(
            functools.partial(attend_kernel, heads),
            grid=(groups,),
            out_shape=[wide_out, jax.ShapeDtypeStruct((total, third), LOW)] + part_outs,
            in_specs=in_specs,
            out_specs=[rows_spec(3 * third), rows_spec(third)] + part_specs,
        )(values, qkv, proj, bias)
    return pl.pallas_call(
        functools.partial(attend_back_kernel, heads),
        grid=(groups,),
        out_shape=[wide_out] + part_outs,
        in_specs=in_specs + [rows_spec(3 * third)],
        out_specs=[rows_spec(3 * third)] + part_specs,
        scratch_shapes=[pltpu.VMEM((rows, third), LOW)],
    )(values, qkv, proj, bias, combined)


def tile_call(body, outs, tiled, whole):
    rows = tiled[0].shape[0]
    block = min(rows, 128)
    count = len(tiled) + len(whole)

    def kernel(*refs):
        results = body(*[ref[...] for ref in refs[:count]])
        for ref, result in zip(refs[count:], results):
            ref[...] = result

    def rows_spec(cols):
        return pl.BlockSpec((block, cols), lambda i: (i, 0))

    return pl.pallas_call(
        kernel,
        grid=(rows // block,),
        out_shape=[jax.ShapeDtypeStruct((rows, cols), dtype) for cols, dtype in outs],
        in_specs=[rows_spec(t.shape[1]) for t in tiled]
        + [pl.BlockSpec(t.shape, lambda i: (0, 0)) for t in whole],
        out_specs=[rows_spec(cols) for cols, _ in outs],
    )(*tiled, *whole)


def cross(lefts, rights):
    out = dot_cross(lefts[0], rights[0])
    for left, right in zip(lefts[1:], rights[1:]):
        out = out + dot_cross(left, right)
    return out.astype(LOW)


def place(gathered, index, order, plans):
    count, _, own, _ = gathered.shape

    def kernel(index_ref, in_ref, *out_refs):
        for j in range(count):
            offset = index_ref[0] ^ j
            entry = 0
            for position, k in enumerate(order):
                entry = jnp.where(offset == k, position, entry)
            for (group, first, pieces, chunk), out_ref in zip(plans, out_refs):
                if chunk is None:
                    out_ref[j * own : (j + 1) * own, :] = in_ref[entry, group].astype(F32)
                    continue
                for p in range(pieces):
                    at = (p * count + j) * chunk
                    low = first + p * chunk
                    out_ref[:, at : at + chunk] = in_ref[
                        entry, group, :, low : low + chunk
                    ].astype(F32)

    shapes = [
        (count * own, gathered.shape[3]) if chunk is None else (own, pieces * count * chunk)
        for _, _, pieces, chunk in plans
    ]
    return pl.pallas_call(
        kernel,
        out_shape=[jax.ShapeDtypeStruct(shape, F32) for shape in shapes],
        in_specs=[SMEM_SPEC, VMEM_SPEC],
        out_specs=[VMEM_SPEC] * len(plans),
    )(index.reshape(1), gathered)


def norm_stats(values):
    return lax.rsqrt(jnp.mean(values * values, -1, keepdims=True) + EPS)


def norm_back(values, scale, gain, grad):
    weighted = grad * gain
    inner = jnp.mean(weighted * values, -1, keepdims=True)
    return scale * (weighted - values * (scale * scale) * inner)


def gelu_parts(v):
    root = 0.7978845608028654
    inner = jnp.tanh(root * (v + 0.044715 * v * v * v))
    value = 0.5 * v * (1.0 + inner)
    slope = 0.5 * (1.0 + inner) + 0.5 * v * (1.0 - inner * inner) * root * (
        1.0 + 3.0 * 0.044715 * v * v
    )
    return value, slope


def make_device(wide, narrow):
    wide_bits = bits_of(wide)
    narrow_bits = bits_of(narrow)
    order_a = list(wide_bits)
    order_c = wide_bits[-1:] + wide_bits[:-1]
    near_order = order_of(narrow_bits)

    def per_device(
        tokens,
        segment_ids,
        routed_index,
        out_grad,
        dense_attn_gain,
        dense_qkv,
        dense_proj,
        dense_mlp_gain,
        dense_up,
        dense_down,
        routed_attn_gain,
        routed_qkv,
        routed_proj,
        routed_mlp_gain,
        routed_up,
        routed_down,
        router_vector,
    ):
        links = Links({"wide": wide, "narrow": narrow})
        w = lax.axis_index("wide").astype(I32)
        n = lax.axis_index("narrow").astype(I32)
        inputs = tokens[0].astype(F32)
        rows, width = inputs.shape
        segments = segment_ids[0]
        chosen = routed_index[0]
        cap = chosen.shape[0]
        heads = HEADS // narrow
        own = width // wide
        ffn = dense_up.shape[1]
        part = width // narrow
        unit = ffn // (wide * narrow)

        def pack_some(shards, kinds):
            def up_of(member):
                shard = shards[member].reshape(own, wide, narrow, unit)
                piece = lax.dynamic_index_in_dim(shard, n, 2, keepdims=False)
                return piece.reshape(own, ffn // narrow)

            def down_of(member):
                shard = shards[member].reshape(narrow, unit, width)
                return lax.dynamic_index_in_dim(shard, n, 0, keepdims=False)

            def attn_of(member):
                mixed = jnp.concatenate([shards[member], shards[member + 1]], 1)
                mixed = mixed.reshape(own, 4, narrow, part)
                piece = lax.dynamic_index_in_dim(mixed, n, 2, keepdims=False)
                return piece.reshape(own, 4 * part)

            layouts, pieces, member = [], [], 0
            for kind in kinds:
                if kind == "a":
                    members = [(member, 3, part), (member + 1, 1, part)]
                    layouts.append(((own, 4 * part), members))
                    pieces.append(lambda m=member: attn_of(m))
                elif kind == "u":
                    layouts.append(((own, ffn // narrow), [(member, wide, unit)]))
                    pieces.append(lambda m=member: up_of(m))
                else:
                    layouts.append(((unit, width), [(member, None, None)]))
                    pieces.append(lambda m=member: down_of(m))
                member += 2 if kind == "a" else 1
            if unit % 128 == 0:
                return pack(n, narrow, shards, layouts)
            return [piece()[None] for piece in pieces]

        def swap_blocks(array, axis):
            got = []
            for k in range(narrow):
                block = lax.dynamic_slice_in_dim(array, (n ^ k) * part, part, axis)
                got.append(block if k == 0 else links.swap(block, "narrow", k))
            return got

        def open_proj(proj_cols):
            return xor_blocks(jnp.concatenate(swap_blocks(proj_cols, 0), 1), n, narrow, 1)

        def open_rows(parts, columns):
            return assemble([(parts, [(0, columns, 0, 0)])], w, (columns,))[0]

        def proj_columns(proj_grad):
            return xor_blocks(jnp.concatenate(swap_blocks(proj_grad, 1), 0), n, narrow, 0)

        def flat(array):
            return array.reshape(-1, array.shape[-1])

        def share_core(local):
            return jnp.concatenate([local, links.swap(local, "narrow", 1)], 0)

        def swap_far(local):
            return links.swap(local, "narrow", 2)

        def share(local):
            got = [local] + [links.swap(local, "narrow", k) for k in range(1, narrow)]
            return jnp.stack(got, 0)

        def total(whole):
            parts = whole.reshape(narrow, -1, width)
            out = parts[0].astype(F32)
            for k in range(1, narrow):
                out = out + links.swap(parts[k], "narrow", k).astype(F32)
            return out

        def total_core(keep, send):
            return keep.astype(F32) + links.swap(send, "narrow", 1).astype(F32)

        def total_far(keep, send):
            return swap_far(total_core(keep, send).astype(LOW))

        def halves(chunk):
            half = chunk.shape[0] // 2
            return chunk[:half], chunk[half:]

        def normed_of(values, scale, gain):
            return (values * scale * gain).astype(LOW)

        def up_body(normed, up):
            pre = dot_rows(normed, up)
            return pre, gelu_parts(pre)[0].astype(LOW)

        def both_body(normed, grad, up, down):
            pre = dot_rows(normed, up)
            value, slope = gelu_parts(pre)
            active = value.astype(LOW)
            pre_grad = (slope * dot_back(grad, down)).astype(LOW)
            part = dot_back(pre_grad, up).astype(LOW)
            return active, dot_rows(active, down).astype(LOW), pre_grad, part

        def gain_grad(weight, grad, gain):
            return jnp.sum(weight.astype(F32) * grad, -1) / gain.astype(F32)

        unit_all = ffn // narrow

        (piece_a,) = pack_some([dense_qkv, dense_proj], "a")
        split = 2 * part
        get_a = Gather(links, piece_a[:, :, :split], order_a)
        get_b = Gather(links, piece_a[:, :, split:], order_c)
        get_a.next()
        get_b.next()
        gains = jnp.stack([dense_attn_gain, dense_mlp_gain, routed_attn_gain, routed_mlp_gain])
        gains = links.gather(gains[None], "wide", order_a[:1])
        (gains,) = sync([get_a, get_b], gains)

        get_a.next(2)
        get_b.next()
        gains = links.gather(gains, "wide", order_a[1:])
        marks = share(jnp.concatenate([segments, chosen, jnp.take(segments, chosen)]))
        scale_0 = norm_stats(inputs)
        piece_u, piece_d, *pieces_r = pack_some(
            [dense_up, dense_down, routed_qkv, routed_proj, routed_up, routed_down], "udaud"
        )
        get_u = Gather(links, piece_u, order_a)
        get_d = Gather(links, piece_d, order_a)
        everything = [get_a, get_b, get_u, get_d]
        gains, scale_0, marks = sync(everything, gains, scale_0, marks)

        get_a.next()
        get_b.next(2)
        get_u.next()
        spread = order_of(order_a)
        places = jnp.array([spread.index(k) for k in range(wide)], I32)
        gains = jnp.take(gains, places[w ^ jnp.arange(wide, dtype=I32)], axis=0)
        gains = gains.transpose(1, 0, 2).reshape(4, width).astype(F32)
        normed = normed_of(inputs, scale_0, gains[0])
        far = swap_far(normed)
        normed_0 = [share_core(normed)]
        seg_all = marks[:, :rows]
        pos_r = marks[:, rows : rows + cap]
        seg_r = marks[:, rows + cap :].reshape(-1)
        where_r, of_r = pos_r.reshape(-1), jnp.repeat(jnp.arange(narrow, dtype=I32), cap)
        pos = jnp.arange(rows, dtype=I32)
        allowed = (pos[None, None, :] <= pos[None, :, None]) & (
            seg_all[:, None, :] == seg_all[:, :, None]
        )
        bias_0 = jnp.where(allowed, 0.0, NEG).astype(F32)
        bias_0 = [bias_0[: narrow // 2], bias_0[narrow // 2 :]]
        allowed = (where_r[None, :] <= where_r[:, None]) & (seg_r[None, :] == seg_r[:, None])
        allowed = allowed & (of_r[None, :] == of_r[:, None])
        bias_r = jnp.where(allowed, 0.0, NEG).astype(F32)[None]
        hits_all = (pos[None, :, None] == pos_r[:, None, :]).astype(LOW)
        gains, far, normed_0, bias_0, bias_r, hits_all, pieces_r = sync(
            everything, gains, far, normed_0, bias_0, bias_r, hits_all, pieces_r
        )
        full_ra, up_r, down_r = [
            lax.all_gather(piece[0], "wide", axis=0, tiled=True) for piece in pieces_r
        ]

        get_u.next(2)
        normed_0.append(share_core(far))
        qkv_d, proj_d = assemble(
            [
                (get_a.finish(), [(0, split, 0, 0)]),
                (get_b.finish(), [(0, part, 0, split), (part, 2 * part, 1, 0)]),
            ],
            w,
            (3 * part, part),
        )
        proj_d = open_proj(proj_d)
        second = attend_call(heads, normed_0[1], qkv_d, proj_d, bias_0[1])
        everything = [get_u, get_d]
        second, qkv_d, proj_d = sync(everything, second, qkv_d, proj_d)

        get_u.next()
        get_d.next()
        far = total_far(*second[2:])
        first = attend_call(heads, normed_0[0], qkv_d, proj_d, bias_0[0])
        combined_0 = [first[0], second[0]]
        attended_0 = [first[1], second[1]]
        near = total_core(*first[2:])
        near, far = sync(everything, near, far)

        get_d.next(2)
        hidden = inputs + near + far.astype(F32)
        scale_1 = norm_stats(hidden)
        normed = normed_of(hidden, scale_1, gains[1])
        far = swap_far(normed)
        normed_1 = [share_core(normed)]
        up_d = open_rows(get_u.finish(), unit_all)
        everything = everything[1:]
        first = tile_call(up_body, [(unit_all, F32), (unit_all, LOW)], normed_1, [up_d])
        first, far, up_d, hidden, scale_1 = sync(everything, first, far, up_d, hidden, scale_1)

        get_d.next()
        normed_1.append(share_core(far))
        second = tile_call(up_body, [(unit_all, F32), (unit_all, LOW)], [normed_1[1]], [up_d])
        pre_1 = [first[0], second[0]]
        active_1 = [first[1], second[1]]
        active_1, pre_1 = sync(everything, active_1, pre_1)

        down_d = open_rows(get_d.finish(), width)
        far = total_far(*[dot_rows(a, down_d).astype(LOW) for a in halves(active_1[1])])
        near = total_core(*[dot_rows(a, down_d).astype(LOW) for a in halves(active_1[0])])
        near, far, down_d = sync([], near, far, down_d)

        middle = hidden + near + far.astype(F32)
        selected = jnp.take(middle, chosen, axis=0)
        route_vec = router_vector.astype(F32)
        rate = jax.nn.sigmoid(jnp.dot(selected, route_vec, precision=HIGH))
        result_grad = out_grad[0]
        picked_grad = jnp.take(result_grad, chosen, axis=0).astype(F32)
        change_grad = rate[:, None] * picked_grad
        scale_2 = norm_stats(selected)
        normed_2 = flat(share(normed_of(selected, scale_2, gains[2])))
        qkv_r, proj_r = full_ra[:, : 3 * part], open_proj(full_ra[:, 3 * part :])
        combined_2, attended_2, part_2 = attend_call(heads, normed_2, qkv_r, proj_r, bias_r)
        routed_att = total(part_2)
        grad_3 = flat(share(change_grad.astype(LOW)))
        after = selected + routed_att
        scale_3 = norm_stats(after)
        normed_3 = flat(share(normed_of(after, scale_3, gains[3])))
        grad_1 = [share_core(result_grad), share_core(swap_far(result_grad))]

        active_3, routed_out, pre_grad_3, normed_part = tile_call(
            both_body,
            [(unit_all, LOW), (width, LOW), (unit_all, LOW), (width, LOW)],
            [normed_3, grad_3],
            [up_r, down_r],
        )
        both_r = jnp.concatenate(
            [cross([normed_3], [pre_grad_3]), cross([active_3], [grad_3])], 1
        )
        both_r, normed_part, routed_out, grad_1 = sync(
            [], both_r, normed_part, routed_out, grad_1
        )
        shard_r = lax.psum_scatter(both_r, "wide", scatter_dimension=0, tiled=True)

        after_grad = norm_back(after, scale_3, gains[3], total(normed_part))
        grad_2 = flat(share((change_grad + after_grad).astype(LOW)))
        proj_grad = proj_columns(cross([attended_2], [grad_2]))
        combined_grad_2, part_2 = attend_call(heads, grad_2, qkv_r, proj_r, bias_r, combined_2)
        change = routed_att + total(routed_out)
        put_ra = Scatter(links, [cross([normed_2], [combined_grad_2]), proj_grad], w, order_a)
        part_2, change = sync([put_ra], part_2, change)

        put_ra.next()
        rate_grad = jnp.sum(picked_grad * change, -1)
        logit_grad = rate_grad * rate * (1.0 - rate)
        att_in_grad = norm_back(selected, scale_2, gains[2], total(part_2))
        selected_grad = after_grad + att_in_grad + logit_grad[:, None] * route_vec[None, :]
        fresh = share((picked_grad + selected_grad).astype(LOW))
        router_total = jnp.dot(logit_grad, selected, precision=HIGH)
        hops = [("wide", bit) for bit in wide_bits[:-1]]
        hops += [("narrow", bit) for bit in narrow_bits[::-1]] + [("wide", wide_bits[-1])]

        def hop(value):
            if hops:
                value = value + links.swap(value, *hops.pop(0))
            return value

        router_total = hop(router_total)
        placed = jnp.einsum("sqk,skd->sqd", hits_all, fresh, preferred_element_type=F32)
        taken = jnp.any(hits_all != 0, -1, keepdims=True)
        half = narrow // 2
        grad_1 = [
            flat(jnp.where(taken[i * half : (i + 1) * half],
                           placed[i * half : (i + 1) * half].astype(LOW),
                           base.reshape(half, rows, width)))
            for i, base in enumerate(grad_1)
        ]
        put_d = Scatter(links, [cross(active_1, grad_1)], w, order_a)
        grad_1, selected_grad, router_total = sync([put_d], grad_1, selected_grad, router_total)

        put_d.next()

        def back_ffn(i):
            grad = dot_back(grad_1[i], down_d)
            pre_grad = (gelu_parts(pre_1[i])[1] * grad).astype(LOW)
            return pre_grad, dot_back(pre_grad, up_d).astype(LOW)

        second = back_ffn(1)
        far = total_far(*halves(second[1]))
        first = back_ffn(0)
        near = total_core(*halves(first[1]))
        pre_grad_1 = [first[0], second[0]]
        put_u = Scatter(links, [cross(normed_1, pre_grad_1)], w, order_a)
        router_total = hop(router_total)
        near, far, router_total = sync([put_u], near, far, router_total)

        put_u.next()
        hits = (pos[:, None] == chosen[None, :]).astype(F32)
        middle_grad = result_grad.astype(F32) + jnp.dot(hits, selected_grad, precision=HIGH)
        hidden_grad = middle_grad + norm_back(
            hidden, scale_1, gains[1], near + far.astype(F32)
        )
        hidden_low = hidden_grad.astype(LOW)
        far = swap_far(hidden_low)
        grad_0 = [share_core(hidden_low)]
        first = attend_call(heads, grad_0[0], qkv_d, proj_d, bias_0[0], combined_0[0])
        router_total = hop(router_total)
        moving = [put_ra, put_d]
        first, far, hidden_grad, router_total = sync(
            moving, first, far, hidden_grad, router_total
        )

        def around(shards):
            gathered = links.gather(jnp.stack(shards)[None], "narrow", narrow_bits[:-1])
            return links.gather(gathered, "narrow", narrow_bits[-1:])

        put_d.next()
        put_ra.next()
        grad_0.append(share_core(far))
        second = attend_call(heads, grad_0[1], qkv_d, proj_d, bias_0[1], combined_0[1])
        proj_grad = proj_columns(cross(attended_0, grad_0))
        combined_grad_0 = [first[0], second[0]]
        put_a = Scatter(links, [cross(normed_0, combined_grad_0), proj_grad], w, order_a)
        router_total = hop(router_total)
        moving = [put_ra, put_d, put_u, put_a]
        first, second, router_total = sync(moving, first[1:], second[1:], router_total)

        put_a.next()
        put_u.next()
        put_d.next()
        put_ra.next()
        far = total_far(*second)
        near = total_core(*first)
        done_rf = around([shard_r[:, :unit_all], shard_r[:, unit_all:]])
        plans_f = [(0, 0, wide, unit), (1, 0, 1, None)]
        plans_a = [(0, 0, 3, part), (0, 3 * part, 1, part)]
        input_part = norm_back(inputs, scale_0, gains[0], near + far.astype(F32))
        input_total = (hidden_grad + input_part).astype(LOW)
        added = jnp.dot(hits, rate[:, None] * change, precision=HIGH)
        result = (middle + added).astype(LOW)
        moving = [put_ra, put_d, put_u, put_a]
        input_total, result, router_total = sync(moving, input_total, result, router_total)

        put_a.next()
        put_u.next()
        while hops:
            router_total = hop(router_total)
        done_ra = around([put_ra.finish()])
        done_dd = around([put_d.finish()])
        out_up_r, out_down_r = place(done_rf, n, near_order, plans_f)
        gain_ru = gain_grad(routed_up, out_up_r, routed_mlp_gain)
        (gain_ru,) = sync([put_a, put_u], gain_ru)

        put_a.next()
        done_du = around([put_u.finish()])
        out_qkv_r, out_proj_r = place(done_ra, n, near_order, plans_a)
        gain_ra = gain_grad(routed_qkv, out_qkv_r, routed_attn_gain)
        (out_down,) = place(done_dd, n, near_order, [(0, 0, 1, None)])
        out_down, gain_ra = sync([put_a], out_down, gain_ra)

        done_a = around([put_a.finish()])
        (out_up,) = place(done_du, n, near_order, [(0, 0, wide, unit)])
        gain_u = gain_grad(dense_up, out_up, dense_mlp_gain)
        done_a, gain_u = sync([], done_a, gain_u)
        out_qkv, out_proj = place(done_a, n, near_order, plans_a)
        return (
            result[None],
            input_total[None],
            gain_grad(dense_qkv, out_qkv, dense_attn_gain),
            out_qkv,
            out_proj,
            gain_u,
            out_up,
            out_down,
            gain_ra,
            out_qkv_r,
            out_proj_r,
            gain_ru,
            out_up_r,
            out_down_r,
            router_total,
        )

    return per_device


def solution(mesh):
    both = P(("wide", "narrow"))
    wide = P("wide")
    weights = (wide,) * 6
    return jax.shard_map(
        make_device(mesh.shape["wide"], mesh.shape["narrow"]),
        mesh=mesh,
        in_specs=(both, both, both, both) + weights + weights + (P(),),
        out_specs=(both, both) + weights + weights + (P(),),
        check_vma=False,
    )
```

time: 592 us -> 545 us (0.921)
  waiting for transfers between devices: 256 us -> 187 us
  matrix products: 73.9 us -> 37.5 us
  Pallas kernels: 54.2 us -> 87.5 us
  other arithmetic: 56.7 us -> 68.8 us
  starting transfers between devices: 88.2 us -> 98.9 us
    ppermute x86 -> x112, waiting for transfers between devices: 256 us -> 187 us  [swap(): lax.ppermute(array, axis, [(i, i ^ bit) for i in range(self.sizes[axis])])]
    dot_general x12 -> x4, matrix products: 31.1 us -> 8.35 us  [dot_rows(): return jnp.dot(left, right, preferred_element_type=F32)]
    dot_general x12 -> x4, matrix products: 22.9 us -> 7.02 us  [dot_back(): lax.dot_general(left, right, (((1,), (1,)), ((), ())), preferred_element_...]
    pallas_call x3 -> x6, Pallas kernels: 9.18 us -> 25 us  [the longest x3 16.2 us: tile_call(): pl.pallas_call(kernel, grid=(rows // block,), out_shape=[jax.ShapeDtypeSt...]
    ppermute x86 -> x112, starting transfers between devices: 87.8 us -> 98.3 us  [swap(): lax.ppermute(array, axis, [(i, i ^ bit) for i in range(self.sizes[axis])])]
    concatenate x15 -> x13, other arithmetic: 1.49 us -> 9.46 us  [gather(): local = jnp.concatenate([local, self.swap(local, axis, bit)], 0)]
    pallas_call x3, Pallas kernels: 17.9 us -> 25 us  [attend_call(): pl.pallas_call(functools.partial(attend_back_kernel, heads), grid=(groups...]
    pallas_call x3, Pallas kernels: 11.2 us -> 18.1 us  [attend_call(): pl.pallas_call(functools.partial(attend_kernel, heads), grid=(groups,), o...]
  transfers between devices with their start and end apart: 90 -> 116, of which waited for: 42 -> 36; matrix products, arithmetic and copies ran while one was open for 24% -> 23% of each run, Pallas kernels for 8% -> 15%
where the time goes in v1:
time: 545 us; the launch traced here: 535 us
  waiting for transfers between devices  187 us (34%)
  starting transfers between devices  98.9 us (18%)
  Pallas kernels  87.5 us (16%)
  other arithmetic  68.8 us (13%)
  local copies, waits for them, and re-layouts  38.5 us (7%)
  matrix products  37.5 us (7%)
  between operations  16.5 us (3%)
    ppermute x112, waiting for transfers between devices, swap(): lax.ppermute(array, axis, [(i, i ^ bit) for i in range(self.sizes[axis])])  187 us
    ppermute x112, starting transfers between devices, swap(): lax.ppermute(array, axis, [(i, i ^ bit) for i in range(self.sizes[axis])])  98.3 us
    pallas_call x3, Pallas kernels, attend_call(): pl.pallas_call(functools.partial(attend_back_kernel, heads), grid=(groups...  25 us
    pallas_call x3, Pallas kernels, attend_call(): pl.pallas_call(functools.partial(attend_kernel, heads), grid=(groups,), o...  18.1 us
    dot_general x12, matrix products, dot_cross(): lax.dot_general(left, right, (((0,), (0,)), ((), ())), preferred_element_...  16.9 us
    pallas_call x3, Pallas kernels, tile_call(): pl.pallas_call(kernel, grid=(rows // block,), out_shape=[jax.ShapeDtypeSt...  16.2 us
    pallas_call x5, Pallas kernels, place(): pl.pallas_call(kernel, out_shape=[jax.ShapeDtypeStruct(shape, F32) for sh...  15.1 us
    unnamed x248, local copies, waits for them, and re-layouts  11.7 us
  transfers between devices with their start and end apart: 116, of which 36 were waited for; matrix products, arithmetic and copies ran while one was open for 23% of the time, Pallas kernels for 15%

profile of v1, /device:TPU:0, one launch (start us, length us, event | category | flops | bytes accessed | tf_op | source)
XLA Modules:
  0.0 534.5 jit_solution(13311676319486876780)
XLA Ops:
  18.5 2.7 collective-permute-start.2
  25.7 5.4 %collective-permute-done = bf16[1,128,512]{2,1,0:T(8,128)(2,1)S(1)} collective-permute-done((bf16[1,128,512]{2,1,0:T(8,128)(2,1)S(1)}, bf16[1,128,512]{2,1,0:T(8,128)(2,1)S(1)}, u32[]{:S(2)}, u32[]{:S(2)}) %collective-permute-start) | collective-permute-done | bytes 131104 | tf_op jit(solution)/shard_map/ppermute | solution.py:59
  42.5 5.1 collective-permute-done.3.refs_1_
  53.9 4.1 collective-permute-start.12
  60.2 5.3 collective-permute-done.14
  67.7 5.3 collective-permute-done.13.refs_7_
  73.7 3.1 shard_map.291
  82.2 2.7 collective-permute-done.20
  84.9 3.5 collective-permute-start.18
  91.7 6.9 %shard_map.292 = (bf16[512,768]{1,0:T(8,128)(2,1)}, bf16[512,256]{1,0:T(8,128)(2,1)}, bf16[256,1024]{1,0:T(8,128)(2,1)}, bf16[256,1024]{1,0:T(8,128)(2,1)}) custom-call(bf16[512,1024]{1,0:T(8,128)(2,1)} %copy-done.3, bf16[1024,768]{1,0:T(8,128)(2,1)} %get-tuple-element.231.qkv_ref, bf16[256,1024]{1,0:T(8,128)(2,1)} %maximum_select_fusion.1.proj_ref, ...), custom_call_target="tpu_custom_call" | custom-call | tf_op jit(solution)/shard_map/pallas_call | solution.py:319
  98.6 4.8 collective-permute-done.17.refs_1_
  103.6 7.1 %shard_map.293 = (bf16[512,768]{1,0:T(8,128)(2,1)}, bf16[512,256]{1,0:T(8,128)(2,1)}, bf16[256,1024]{1,0:T(8,128)(2,1)}, bf16[256,1024]{1,0:T(8,128)(2,1)}) custom-call(bf16[512,1024]{1,0:T(8,128)(2,1)} %pad_maximum_fusion.2.normed_ref, bf16[1024,768]{1,0:T(8,128)(2,1)} %get-tuple-element.231.qkv_ref, bf16[256,1024]{1,0:T(8,128)(2,1)} %maximum_select_fusion.1.proj_ref, ...), custom_call_target="tpu_custom_call" | custom-call | tf_op jit(solution)/shard_map/pallas_call | solution.py:319
  111.1 2.6 collective-permute-start.24
  116.8 21.3 %collective-permute-done.24 = bf16[1,128,1024]{2,1,0:T(8,128)(2,1)S(1)} collective-permute-done((bf16[1,128,1024]{2,1,0:T(8,128)(2,1)S(1)}, bf16[1,128,1024]{2,1,0:T(8,128)(2,1)S(1)}, u32[]{:S(2)}, u32[]{:S(2)}) %collective-permute-start.24) | collective-permute-done | bytes 262176 | tf_op jit(solution)/shard_map/ppermute | solution.py:59
  143.0 2.9 shard_map.294.refs_1_
  147.8 5.5 %shard_map.295 = (f32[512,1024]{1,0:T(8,128)}, bf16[512,1024]{1,0:T(8,128)(2,1)}) custom-call(bf16[512,1024]{1,0:T(8,128)(2,1)} %pad_maximum_fusion.3.refs_0_, bf16[1024,1024]{1,0:T(8,128)(2,1)} %shard_map.294.refs_1_), custom_call_target="tpu_custom_call" | custom-call | tf_op jit(solution)/shard_map/pallas_call | solution.py:349
  154.2 7.1 %collective-permute-done.28.refs_1_ = bf16[2,128,1024]{2,1,0:T(8,128)(2,1)} collective-permute-done((bf16[2,128,1024]{2,1,0:T(8,128)(2,1)S(1)}, bf16[2,128,1024]{2,1,0:T(8,128)(2,1)}, u32[]{:S(2)}, u32[]{:S(2)}) %collective-permute-start.28) | collective-permute-done | bytes 524320 | tf_op jit(solution)/shard_map/ppermute | solution.py:59
  161.3 3.7 collective-permute-start.32
  169.8 5.3 shard_map.296
  175.1 11.3 %collective-permute-done.32.refs_3_ = bf16[2,128,1024]{2,1,0:T(8,128)(2,1)} collective-permute-done((bf16[2,128,1024]{2,1,0:T(8,128)(2,1)}, bf16[2,128,1024]{2,1,0:T(8,128)(2,1)}, u32[]{:S(2)}, u32[]{:S(2)}) %collective-permute-start.32) | collective-permute-done | bytes 524320 | tf_op jit(solution)/shard_map/ppermute | solution.py:59
  186.5 2.9 shard_map.297
  189.4 3.4 convolution_convert_fusion.6
  201.7 12.5 %collective-permute-done.36 = bf16[256,1024]{1,0:T(8,128)(2,1)S(1)} collective-permute-done((bf16[256,1024]{1,0:T(8,128)(2,1)S(1)}, bf16[256,1024]{1,0:T(8,128)(2,1)S(1)}, u32[]{:S(2)}, u32[]{:S(2)}) %collective-permute-start.36) | collective-permute-done | bytes 524320 | tf_op jit(solution)/shard_map/ppermute | solution.py:59
  229.2 4.1 shard_map.298
  251.4 5.3 %shard_map.299 = (bf16[128,1024]{1,0:T(8,128)(2,1)}, bf16[128,1024]{1,0:T(8,128)(2,1)}, bf16[128,1024]{1,0:T(8,128)(2,1)}, bf16[128,1024]{1,0:T(8,128)(2,1)}) custom-call(bf16[128,1024]{1,0:T(8,128)(2,1)} %bitcast.251, bf16[128,1024]{1,0:T(8,128)(2,1)} %bitcast.249, bf16[1024,1024]{1,0:T(8,128)(2,1)} %bitcast.263, bf16[1024,1024]{1,0:T(8,128)(2,1)} %bitcast.264), custom_call_target="tpu_custom_call" | custom-call | tf_op jit(solution)/shard_map/pallas_call | solution.py:349
  281.2 5.3 shard_map.300
  292.7 2.8 collective-permute-done.69
  323.7 2.7 add_convert_fusion
  326.6 9.8 %collective-permute-done.78 = bf16[256,1024]{1,0:T(8,128)(2,1)S(1)} collective-permute-done((bf16[256,1024]{1,0:T(8,128)(2,1)S(1)}, bf16[256,1024]{1,0:T(8,128)(2,1)S(1)}, u32[]{:S(2)}, u32[]{:S(2)}) %collective-permute-start.78) | collective-permute-done | bytes 524320 | tf_op jit(solution)/shard_map/ppermute | solution.py:59
  346.3 10.0 %shard_map.301 = (bf16[512,768]{1,0:T(8,128)(2,1)}, bf16[256,1024]{1,0:T(8,128)(2,1)}, bf16[256,1024]{1,0:T(8,128)(2,1)}) custom-call(bf16[512,1024]{1,0:T(8,128)(2,1)} %pad_maximum_fusion.7.grad_ref, bf16[1024,768]{1,0:T(8,128)(2,1)} %get-tuple-element.231.qkv_ref, bf16[256,1024]{1,0:T(8,128)(2,1)} %maximum_select_fusion.1.proj_ref, ...), custom_call_target="tpu_custom_call" | custom-call | tf_op jit(solution)/shard_map/pallas_call | solution.py:326
  356.3 9.9 %collective-permute-done.75 = bf16[2,2,128,1024]{3,2,0,1:T(8,128)(2,1)} collective-permute-done((bf16[2,2,128,1024]{3,2,0,1:T(8,128)(2,1)}, bf16[2,2,128,1024]{3,2,0,1:T(8,128)(2,1)}, u32[]{:S(2)}, u32[]{:S(2)}) %collective-permute-start.75) | collective-permute-done | bytes 1048608 | tf_op jit(solution)/shard_map/ppermute | solution.py:59
  378.3 9.8 %shard_map.302 = (bf16[512,768]{1,0:T(8,128)(2,1)}, bf16[256,1024]{1,0:T(8,128)(2,1)}, bf16[256,1024]{1,0:T(8,128)(2,1)}) custom-call(bf16[512,1024]{1,0:T(8,128)(2,1)} %copy-done.13, bf16[1024,768]{1,0:T(8,128)(2,1)} %get-tuple-element.231.qkv_ref, bf16[256,1024]{1,0:T(8,128)(2,1)} %maximum_select_fusion.1.proj_ref, ...), custom_call_target="tpu_custom_call" | custom-call | tf_op jit(solution)/shard_map/pallas_call | solution.py:326
  393.9 12.0 %collective-permute-done.83 = bf16[2,128,1024]{2,1,0:T(8,128)(2,1)S(1)} collective-permute-done((bf16[2,128,1024]{2,1,0:T(8,128)(2,1)}, bf16[2,128,1024]{2,1,0:T(8,128)(2,1)S(1)}, u32[]{:S(2)}, u32[]{:S(2)}) %collective-permute-start.83) | collective-permute-done | bytes 524320 | tf_op jit(solution)/shard_map/ppermute | solution.py:59
  413.9 3.0 collective-permute-start.92
  417.2 8.7 %collective-permute-done.97 = bf16[256,1024]{1,0:T(8,128)(2,1)S(1)} collective-permute-done((bf16[256,1024]{1,0:T(8,128)(2,1)S(1)}, bf16[256,1024]{1,0:T(8,128)(2,1)S(1)}, u32[]{:S(2)}, u32[]{:S(2)}) %collective-permute-start.97) | collective-permute-done | bytes 524320 | tf_op jit(solution)/shard_map/ppermute | solution.py:59
  427.7 2.6 collective-permute-done.92
  430.3 9.2 %collective-permute-done.91 = bf16[128,1024]{1,0:T(8,128)(2,1)S(1)} collective-permute-done((bf16[128,1024]{1,0:T(8,128)(2,1)S(1)}, bf16[128,1024]{1,0:T(8,128)(2,1)S(1)}, u32[]{:S(2)}, u32[]{:S(2)}) %collective-permute-start.91) | collective-permute-done | bytes 262176 | tf_op jit(solution)/shard_map/ppermute | solution.py:59
  446.3 15.0 %collective-permute-done.100 = bf16[1,2,128,1024]{3,2,1,0:T(8,128)(2,1)S(1)} collective-permute-done((bf16[1,2,128,1024]{3,2,1,0:T(8,128)(2,1)S(1)}, bf16[1,2,128,1024]{3,2,1,0:T(8,128)(2,1)S(1)}, u32[]{:S(2)}, u32[]{:S(2)}) %collective-permute-start.100) | collective-permute-done | bytes 524320 | tf_op jit(solution)/shard_map/ppermute | solution.py:59
  470.2 2.7 shard_map.305
  475.0 2.8 shard_map.304
  479.4 2.7 pad_maximum_fusion.1.in_ref
  482.2 4.1 shard_map.303
  493.1 5.2 collective-permute-done.109
  498.4 8.3 %collective-permute-done.102 = bf16[128,1024]{1,0:T(8,128)(2,1)S(1)} collective-permute-done((bf16[128,1024]{1,0:T(8,128)(2,1)S(1)}, bf16[128,1024]{1,0:T(8,128)(2,1)S(1)}, u32[]{:S(2)}, u32[]{:S(2)}) %collective-permute-start.102) | collective-permute-done | bytes 262176 | tf_op jit(solution)/shard_map/ppermute | solution.py:59
  507.7 3.6 collective-permute-done.111
  511.9 3.1 collective-permute-done.107
  516.3 2.9 shard_map.306
  522.7 2.7 shard_map.307
  (654 shorter events, 235.2 us)
Async XLA Ops:
  7.2 211.5 %all-gather.7.cloned.1.call-start = ((), (), s32[]{:S(2)}) async-start(), calls=%async_computation.2 | async-start | bytes 2359296 | tf_op jit(solution)/shard_map/all_gather | solution.py:608
  10.8 23.7 %collective-permute-start.8 = (s32[320]{0:T(512)S(1)}, s32[320]{0:T(512)S(1)}, u32[]{:S(2)}, u32[]{:S(2)}) collective-permute-start(s32[320]{0:T(512)S(1)} %pad_add_fusion.1), channel_id=1, source_target_pairs={{0,1},{1,0},{2,3},{3,2},{4,5},{5,4},{6,7},{7,6},{8,9},{9,8},{10,11... | collective-permute-start | bytes 3848 | tf_op jit(solution)/shard_map/ppermute | solution.py:59
  11.3 23.2 %collective-permute-start.9 = (s32[320]{0:T(512)S(1)}, s32[320]{0:T(512)S(1)}, u32[]{:S(2)}, u32[]{:S(2)}) collective-permute-start(s32[320]{0:T(512)S(1)} %pad_add_fusion.1), channel_id=1, source_target_pairs={{0,2},{1,3},{2,0},{3,1},{4,6},{5,7},{6,4},{7,5},{8,10},{9,11},{10,... | collective-permute-start | bytes 3848 | tf_op jit(solution)/shard_map/ppermute | solution.py:59
  13.9 20.7 %collective-permute-start.10 = (s32[320]{0:T(512)S(1)}, s32[320]{0:T(512)S(1)}, u32[]{:S(2)}, u32[]{:S(2)}) collective-permute-start(s32[320]{0:T(512)S(1)} %pad_add_fusion.1), channel_id=1, source_target_pairs={{0,3},{1,2},{2,1},{3,0},{4,7},{5,6},{6,5},{7,4},{8,11},{9,10},{10,... | collective-permute-start | bytes 3848 | tf_op jit(solution)/shard_map/ppermute | solution.py:59
  48.4 18.1 %collective-permute-start.16 = (bf16[256,1024]{1,0:T(8,128)(2,1)S(1)}, bf16[256,1024]{1,0:T(8,128)(2,1)S(1)}, u32[]{:S(2)}, u32[]{:S(2)}) collective-permute-start(bf16[256,1024]{1,0:T(8,128)(2,1)S(1)} %fusion.30), channel_id=1, source_target_pairs={{0,1},{1,0},{2,3},{3,2},{4,5},{5,4},{6,7},{7,6},{8,9},{9,8},{10,11... | collective-permute-start | bytes 1572872 | tf_op jit(solution)/shard_map/ppermute | solution.py:59
  48.5 24.4 %collective-permute-start.15 = (bf16[256,1024]{1,0:T(8,128)(2,1)S(1)}, bf16[256,1024]{1,0:T(8,128)(2,1)}, u32[]{:S(2)}, u32[]{:S(2)}) collective-permute-start(bf16[256,1024]{1,0:T(8,128)(2,1)S(1)} %fusion.30), channel_id=1, source_target_pairs={{0,2},{1,3},{2,0},{3,1},{4,6},{5,7},{6,4},{7,5},{8,10},{9,11},{10,... | collective-permute-start | bytes 1572872 | tf_op jit(solution)/shard_map/ppermute | solution.py:59
  50.3 15.2 %collective-permute-start.14 = (bf16[1,128,1024]{2,1,0:T(8,128)(2,1)}, bf16[1,128,1024]{2,1,0:T(8,128)(2,1)S(1)}, u32[]{:S(2)}, u32[]{:S(2)}) collective-permute-start(bf16[1,128,1024]{2,1,0:T(8,128)(2,1)} %get-tuple-element.200), channel_id=1, source_target_pairs={{0,16},{4,20},{8,24},{12,28},{16,0},{20,4},{24,8},{28,12},{1,17},{... | collective-permute-start | bytes 786440 | tf_op jit(solution)/shard_map/ppermute | solution.py:59
  51.7 15.9 %collective-permute-start.11 = (bf16[2,128,512]{2,1,0:T(8,128)(2,1)S(1)}, bf16[2,128,512]{2,1,0:T(8,128)(2,1)S(1)}, u32[]{:S(2)}, u32[]{:S(2)}) collective-permute-start(bf16[2,128,512]{2,1,0:T(8,128)(2,1)S(1)} %collective-permute-done.3.refs_1_), channel_id=1, source_target_pairs={{0,4},{4,0},{8,12},{12,8},{16,20},{20,16},{24,28},{28,24},{1,5},{5... | collective-permute-start | bytes 786440 | tf_op jit(solution)/shard_map/ppermute | solution.py:59
  53.9 13.8 %collective-permute-start.12 = (bf16[2,128,512]{2,1,0:T(8,128)(2,1)S(1)}, bf16[2,128,512]{2,1,0:T(8,128)(2,1)S(1)}, u32[]{:S(2)}, u32[]{:S(2)}) collective-permute-start(bf16[2,128,512]{2,1,0:T(8,128)(2,1)S(1)} %pad_maximum_fusion.21.refs_4_), channel_id=1, source_target_pairs={{0,8},{4,12},{8,0},{12,4},{16,24},{20,28},{24,16},{28,20},{1,9},{5... | collective-permute-start | bytes 786440 | tf_op jit(solution)/shard_map/ppermute | solution.py:59
  73.0 178.4 %all-gather.9.cloned.1.call-start = ((), (), s32[]{:S(2)}) async-start(), calls=%async_computation.3 | async-start | bytes 2359296 | tf_op jit(solution)/shard_map/all_gather | solution.py:608
  80.7 22.8 %collective-permute-start.17 = (bf16[2,128,1024]{2,1,0:T(8,128)(2,1)S(1)}, bf16[2,128,1024]{2,1,0:T(8,128)(2,1)S(1)}, u32[]{:S(2)}, u32[]{:S(2)}) collective-permute-start(bf16[2,128,1024]{2,1,0:T(8,128)(2,1)S(1)} %pad_maximum_fusion.14.refs_0_), channel_id=1, source_target_pairs={{0,8},{4,12},{8,0},{12,4},{16,24},{20,28},{24,16},{28,20},{1,9},{5... | collective-permute-start | bytes 1572872 | tf_op jit(solution)/shard_map/ppermute | solution.py:59
  84.9 18.6 %collective-permute-start.18 = (bf16[2,128,1024]{2,1,0:T(8,128)(2,1)S(1)}, bf16[2,128,1024]{2,1,0:T(8,128)(2,1)S(1)}, u32[]{:S(2)}, u32[]{:S(2)}) collective-permute-start(bf16[2,128,1024]{2,1,0:T(8,128)(2,1)S(1)} %pad_maximum_fusion.14.refs_0_), channel_id=1, source_target_pairs={{0,4},{4,0},{8,12},{12,8},{16,20},{20,16},{24,28},{28,24},{1,5},{5... | collective-permute-start | bytes 1572872 | tf_op jit(solution)/shard_map/ppermute | solution.py:59
  103.6 147.8 %all-gather.11.cloned.1.call-start = ((), (), s32[]{:S(2)}) async-start(), calls=%async_computation.4 | async-start | bytes 2359296 | tf_op jit(solution)/shard_map/all_gather | solution.py:608
  110.7 27.5 %collective-permute-start.25 = (bf16[256,1024]{1,0:T(8,128)(2,1)}, bf16[256,1024]{1,0:T(8,128)(2,1)S(1)}, u32[]{:S(2)}, u32[]{:S(2)}) collective-permute-start(bf16[256,1024]{1,0:T(8,128)(2,1)} %get-tuple-element.235), channel_id=1, source_target_pairs={{0,1},{1,0},{2,3},{3,2},{4,5},{5,4},{6,7},{7,6},{8,9},{9,8},{10,11... | collective-permute-start | bytes 1572872 | tf_op jit(solution)/shard_map/ppermute | solution.py:59
  111.1 27.0 %collective-permute-start.24 = (bf16[1,128,1024]{2,1,0:T(8,128)(2,1)S(1)}, bf16[1,128,1024]{2,1,0:T(8,128)(2,1)S(1)}, u32[]{:S(2)}, u32[]{:S(2)}) collective-permute-start(bf16[1,128,1024]{2,1,0:T(8,128)(2,1)S(1)} %copy-done.84), channel_id=1, source_target_pairs={{0,16},{4,20},{8,24},{12,28},{16,0},{20,4},{24,8},{28,12},{1,17},{... | collective-permute-start | bytes 786440 | tf_op jit(solution)/shard_map/ppermute | solution.py:59
  113.7 24.6 %collective-permute-start.23 = (bf16[2,128,1024]{2,1,0:T(8,128)(2,1)S(1)}, bf16[2,128,1024]{2,1,0:T(8,128)(2,1)S(1)}, u32[]{:S(2)}, u32[]{:S(2)}) collective-permute-start(bf16[2,128,1024]{2,1,0:T(8,128)(2,1)S(1)} %collective-permute-done.17.refs_1_), channel_id=1, source_target_pairs={{0,4},{4,0},{8,12},{12,8},{16,20},{20,16},{24,28},{28,24},{1,5},{5... | collective-permute-start | bytes 1572872 | tf_op jit(solution)/shard_map/ppermute | solution.py:59
  115.6 23.6 %collective-permute-start.27 = (bf16[256,1024]{1,0:T(8,128)(2,1)S(1)}, bf16[256,1024]{1,0:T(8,128)(2,1)S(1)}, u32[]{:S(2)}, u32[]{:S(2)}) collective-permute-start(bf16[256,1024]{1,0:T(8,128)(2,1)S(1)} %add_convert_fusion.7), channel_id=1, source_target_pairs={{0,2},{1,3},{2,0},{3,1},{4,6},{5,7},{6,4},{7,5},{8,10},{9,11},{10,... | collective-permute-start | bytes 1572872 | tf_op jit(solution)/shard_map/ppermute | solution.py:59
  139.8 14.4 %collective-permute-start.31 = (bf16[256,1024]{1,0:T(8,128)(2,1)S(1)}, bf16[256,1024]{1,0:T(8,128)(2,1)}, u32[]{:S(2)}, u32[]{:S(2)}) collective-permute-start(bf16[256,1024]{1,0:T(8,128)(2,1)S(1)} %multiply_convert_fusion), channel_id=1, source_target_pairs={{0,2},{1,3},{2,0},{3,1},{4,6},{5,7},{6,4},{7,5},{8,10},{9,11},{10,... | collective-permute-start | bytes 1572872 | tf_op jit(solution)/shard_map/ppermute | solution.py:59
  141.0 20.3 %collective-permute-start.28 = (bf16[2,128,1024]{2,1,0:T(8,128)(2,1)S(1)}, bf16[2,128,1024]{2,1,0:T(8,128)(2,1)}, u32[]{:S(2)}, u32[]{:S(2)}) collective-permute-start(bf16[2,128,1024]{2,1,0:T(8,128)(2,1)S(1)} %pad_maximum_fusion.15.refs_0_), channel_id=1, source_target_pairs={{0,8},{4,12},{8,0},{12,4},{16,24},{20,28},{24,16},{28,20},{1,9},{5... | collective-permute-start | bytes 1572872 | tf_op jit(solution)/shard_map/ppermute | solution.py:59
  141.0 20.3 %collective-permute-start.29 = (bf16[2,128,1024]{2,1,0:T(8,128)(2,1)S(1)}, bf16[2,128,1024]{2,1,0:T(8,128)(2,1)}, u32[]{:S(2)}, u32[]{:S(2)}) collective-permute-start(bf16[2,128,1024]{2,1,0:T(8,128)(2,1)S(1)} %pad_maximum_fusion.15.refs_0_), channel_id=1, source_target_pairs={{0,4},{4,0},{8,12},{12,8},{16,20},{20,16},{24,28},{28,24},{1,5},{5... | collective-permute-start | bytes 1572872 | tf_op jit(solution)/shard_map/ppermute | solution.py:59
  161.3 25.1 %collective-permute-start.32 = (bf16[2,128,1024]{2,1,0:T(8,128)(2,1)}, bf16[2,128,1024]{2,1,0:T(8,128)(2,1)}, u32[]{:S(2)}, u32[]{:S(2)}) collective-permute-start(bf16[2,128,1024]{2,1,0:T(8,128)(2,1)} %collective-permute-done.28.refs_1_), channel_id=1, source_target_pairs={{0,4},{4,0},{8,12},{12,8},{16,20},{20,16},{24,28},{28,24},{1,5},{5... | collective-permute-start | bytes 1572872 | tf_op jit(solution)/shard_map/ppermute | solution.py:59
  165.1 55.3 %collective-permute-start.53 = (bf16[256,1024]{1,0:T(8,128)(2,1)S(1)}, bf16[256,1024]{1,0:T(8,128)(2,1)}, u32[]{:S(2)}, u32[]{:S(2)}) collective-permute-start(bf16[256,1024]{1,0:T(8,128)(2,1)S(1)} %bitcast.239), channel_id=1, source_target_pairs={{0,2},{1,3},{2,0},{3,1},{4,6},{5,7},{6,4},{7,5},{8,10},{9,11},{10,... | collective-permute-start | bytes 1572872 | tf_op jit(solution)/shard_map/ppermute | solution.py:59
  165.1 27.7 %collective-permute-start.52 = (bf16[256,1024]{1,0:T(8,128)(2,1)S(1)}, bf16[256,1024]{1,0:T(8,128)(2,1)}, u32[]{:S(2)}, u32[]{:S(2)}) collective-permute-start(bf16[256,1024]{1,0:T(8,128)(2,1)S(1)} %bitcast.240), channel_id=1, source_target_pairs={{0,1},{1,0},{2,3},{3,2},{4,5},{5,4},{6,7},{7,6},{8,9},{9,8},{10,11... | collective-permute-start | bytes 1572872 | tf_op jit(solution)/shard_map/ppermute | solution.py:59
  194.9 246.9 %reduce-scatter.2.cloned.1.call-start = ((), (), s32[]{:S(2)}) async-start(), calls=%async_computation.1 | async-start | bytes 4718592 | tf_op jit(solution)/shard_map/reduce_scatter | solution.py:688
  200.3 13.9 %collective-permute-start.36 = (bf16[256,1024]{1,0:T(8,128)(2,1)S(1)}, bf16[256,1024]{1,0:T(8,128)(2,1)S(1)}, u32[]{:S(2)}, u32[]{:S(2)}) collective-permute-start(bf16[256,1024]{1,0:T(8,128)(2,1)S(1)} %fusion.23), channel_id=1, source_target_pairs={{0,2},{1,3},{2,0},{3,1},{4,6},{5,7},{6,4},{7,5},{8,10},{9,11},{10,... | collective-permute-start | bytes 1572872 | tf_op jit(solution)/shard_map/ppermute | solution.py:59
  300.2 56.1 %collective-permute-start.67 = (bf16[2,2,128,1024]{3,2,0,1:T(8,128)(2,1)}, bf16[2,2,128,1024]{3,2,0,1:T(8,128)(2,1)}, u32[]{:S(2)}, u32[]{:S(2)}) collective-permute-start(bf16[2,2,128,1024]{3,2,0,1:T(8,128)(2,1)} %pad_maximum_fusion.6), channel_id=1, source_target_pairs={{0,4},{4,0},{8,12},{12,8},{16,20},{20,16},{24,28},{28,24},{1,5},{5... | collective-permute-start | bytes 3145736 | tf_op jit(solution)/shard_map/ppermute | solution.py:59
  308.7 17.7 %collective-permute-start.79 = (f32[1024]{0:T(1024)S(1)}, f32[1024]{0:T(1024)S(1)}, u32[]{:S(2)}, u32[]{:S(2)}) collective-permute-start(f32[1024]{0:T(1024)S(1)} %add.411), channel_id=1, source_target_pairs={{0,8},{4,12},{8,0},{12,4},{16,24},{20,28},{24,16},{28,20},{1,9},{5... | collective-permute-start | bytes 12296 | tf_op jit(solution)/shard_map/ppermute | solution.py:59
  318.5 47.8 %collective-permute-start.75 = (bf16[2,2,128,1024]{3,2,0,1:T(8,128)(2,1)}, bf16[2,2,128,1024]{3,2,0,1:T(8,128)(2,1)}, u32[]{:S(2)}, u32[]{:S(2)}) collective-permute-start(bf16[2,2,128,1024]{3,2,0,1:T(8,128)(2,1)} %copy_bitcast_fusion.1), channel_id=1, source_target_pairs={{0,4},{4,0},{8,12},{12,8},{16,20},{20,16},{24,28},{28,24},{1,5},{5... | collective-permute-start | bytes 3145736 | tf_op jit(solution)/shard_map/ppermute | solution.py:59
  322.5 13.9 %collective-permute-start.78 = (bf16[256,1024]{1,0:T(8,128)(2,1)S(1)}, bf16[256,1024]{1,0:T(8,128)(2,1)S(1)}, u32[]{:S(2)}, u32[]{:S(2)}) collective-permute-start(bf16[256,1024]{1,0:T(8,128)(2,1)S(1)} %add_convert_fusion.6), channel_id=1, source_target_pairs={{0,2},{1,3},{2,0},{3,1},{4,6},{5,7},{6,4},{7,5},{8,10},{9,11},{10,... | collective-permute-start | bytes 1572872 | tf_op jit(solution)/shard_map/ppermute | solution.py:59
  338.8 27.5 %collective-permute-start.81 = (bf16[256,1024]{1,0:T(8,128)(2,1)}, bf16[256,1024]{1,0:T(8,128)(2,1)}, u32[]{:S(2)}, u32[]{:S(2)}) collective-permute-start(bf16[256,1024]{1,0:T(8,128)(2,1)} %get-tuple-element.446), channel_id=1, source_target_pairs={{0,2},{1,3},{2,0},{3,1},{4,6},{5,7},{6,4},{7,5},{8,10},{9,11},{10,... | collective-permute-start | bytes 1572872 | tf_op jit(solution)/shard_map/ppermute | solution.py:59
  343.7 62.1 %collective-permute-start.85 = (bf16[2,2,128,1024]{3,2,0,1:T(8,128)(2,1)}, bf16[2,2,128,1024]{3,2,0,1:T(8,128)(2,1)}, u32[]{:S(2)}, u32[]{:S(2)}) collective-permute-start(bf16[2,2,128,1024]{3,2,0,1:T(8,128)(2,1)} %copy_bitcast_fusion), channel_id=1, source_target_pairs={{0,4},{4,0},{8,12},{12,8},{16,20},{20,16},{24,28},{28,24},{1,5},{5... | collective-permute-start | bytes 3145736 | tf_op jit(solution)/shard_map/ppermute | solution.py:59
  369.8 24.0 %collective-permute-start.84 = (bf16[2,128,1024]{2,1,0:T(8,128)(2,1)}, bf16[2,128,1024]{2,1,0:T(8,128)(2,1)S(1)}, u32[]{:S(2)}, u32[]{:S(2)}) collective-permute-start(bf16[2,128,1024]{2,1,0:T(8,128)(2,1)} %dynamic-slice_bitcast_fusion.6), channel_id=1, source_target_pairs={{0,8},{4,12},{8,0},{12,4},{16,24},{20,28},{24,16},{28,20},{1,9},{5... | collective-permute-start | bytes 1572872 | tf_op jit(solution)/shard_map/ppermute | solution.py:59
  376.1 15.4 %collective-permute-start.87 = (bf16[256,256]{1,0:T(8,128)(2,1)S(1)}, bf16[256,256]{1,0:T(8,128)(2,1)S(1)}, u32[]{:S(2)}, u32[]{:S(2)}) collective-permute-start(bf16[256,256]{1,0:T(8,128)(2,1)S(1)} %get-tuple-element.387), channel_id=1, source_target_pairs={{0,2},{1,3},{2,0},{3,1},{4,6},{5,7},{6,4},{7,5},{8,10},{9,11},{10,... | collective-permute-start | bytes 393224 | tf_op jit(solution)/shard_map/ppermute | solution.py:59
  377.1 16.3 %collective-permute-start.88 = (bf16[256,256]{1,0:T(8,128)(2,1)S(1)}, bf16[256,256]{1,0:T(8,128)(2,1)S(1)}, u32[]{:S(2)}, u32[]{:S(2)}) collective-permute-start(bf16[256,256]{1,0:T(8,128)(2,1)S(1)} %get-tuple-element.390), channel_id=1, source_target_pairs={{0,3},{1,2},{2,1},{3,0},{4,7},{5,6},{6,5},{7,4},{8,11},{9,10},{10,... | collective-permute-start | bytes 393224 | tf_op jit(solution)/shard_map/ppermute | solution.py:59
  378.0 15.5 %collective-permute-start.89 = (bf16[256,256]{1,0:T(8,128)(2,1)S(1)}, bf16[256,256]{1,0:T(8,128)(2,1)S(1)}, u32[]{:S(2)}, u32[]{:S(2)}) collective-permute-start(bf16[256,256]{1,0:T(8,128)(2,1)S(1)} %get-tuple-element.388), channel_id=1, source_target_pairs={{0,1},{1,0},{2,3},{3,2},{4,5},{5,4},{6,7},{7,6},{8,9},{9,8},{10,11... | collective-permute-start | bytes 393224 | tf_op jit(solution)/shard_map/ppermute | solution.py:59
  391.5 14.4 %collective-permute-start.83 = (bf16[2,128,1024]{2,1,0:T(8,128)(2,1)}, bf16[2,128,1024]{2,1,0:T(8,128)(2,1)S(1)}, u32[]{:S(2)}, u32[]{:S(2)}) collective-permute-start(bf16[2,128,1024]{2,1,0:T(8,128)(2,1)} %dynamic-slice_bitcast_fusion.7), channel_id=1, source_target_pairs={{0,8},{4,12},{8,0},{12,4},{16,24},{20,28},{24,16},{28,20},{1,9},{5... | collective-permute-start | bytes 1572872 | tf_op jit(solution)/shard_map/ppermute | solution.py:59
  406.7 32.8 %collective-permute-start.94 = (bf16[2,2,128,1024]{3,2,0,1:T(8,128)(2,1)S(1)}, bf16[2,2,128,1024]{3,2,0,1:T(8,128)(2,1)S(1)}, u32[]{:S(2)}, u32[]{:S(2)}) collective-permute-start(bf16[2,2,128,1024]{3,2,0,1:T(8,128)(2,1)S(1)} %pad_maximum_fusion.8), channel_id=1, source_target_pairs={{0,4},{4,0},{8,12},{12,8},{16,20},{20,16},{24,28},{28,24},{1,5},{5... | collective-permute-start | bytes 3145736 | tf_op jit(solution)/shard_map/ppermute | solution.py:59
  410.5 29.0 %collective-permute-start.93 = (bf16[2,128,1024]{2,1,0:T(8,128)(2,1)S(1)}, bf16[2,128,1024]{2,1,0:T(8,128)(2,1)S(1)}, u32[]{:S(2)}, u32[]{:S(2)}) collective-permute-start(bf16[2,128,1024]{2,1,0:T(8,128)(2,1)S(1)} %dynamic-slice_bitcast_fusion.5), channel_id=1, source_target_pairs={{0,8},{4,12},{8,0},{12,4},{16,24},{20,28},{24,16},{28,20},{1,9},{5... | collective-permute-start | bytes 1572872 | tf_op jit(solution)/shard_map/ppermute | solution.py:59
  413.9 16.4 %collective-permute-start.92 = (bf16[128,1024]{1,0:T(8,128)(2,1)S(1)}, bf16[128,1024]{1,0:T(8,128)(2,1)S(1)}, u32[]{:S(2)}, u32[]{:S(2)}) collective-permute-start(bf16[128,1024]{1,0:T(8,128)(2,1)S(1)} %dynamic-slice_bitcast_fusion.12), channel_id=1, source_target_pairs={{0,16},{4,20},{8,24},{12,28},{16,0},{20,4},{24,8},{28,12},{1,17},{... | collective-permute-start | bytes 786440 | tf_op jit(solution)/shard_map/ppermute | solution.py:59
  417.1 22.4 %collective-permute-start.91 = (bf16[128,1024]{1,0:T(8,128)(2,1)S(1)}, bf16[128,1024]{1,0:T(8,128)(2,1)S(1)}, u32[]{:S(2)}, u32[]{:S(2)}) collective-permute-start(bf16[128,1024]{1,0:T(8,128)(2,1)S(1)} %dynamic-slice_bitcast_fusion.13), channel_id=1, source_target_pairs={{0,16},{4,20},{8,24},{12,28},{16,0},{20,4},{24,8},{28,12},{1,17},{... | collective-permute-start | bytes 786440 | tf_op jit(solution)/shard_map/ppermute | solution.py:59
  440.7 48.1 %collective-permute-start.99 = (bf16[128,1024]{1,0:T(8,128)(2,1)}, bf16[128,1024]{1,0:T(8,128)(2,1)}, u32[]{:S(2)}, u32[]{:S(2)}) collective-permute-start(bf16[128,1024]{1,0:T(8,128)(2,1)} %dynamic-slice_bitcast_fusion.9), channel_id=1, source_target_pairs={{0,16},{4,20},{8,24},{12,28},{16,0},{20,4},{24,8},{28,12},{1,17},{... | collective-permute-start | bytes 786440 | tf_op jit(solution)/shard_map/ppermute | solution.py:59
  440.8 21.6 %collective-permute-start.105 = (bf16[1,1,128,1024]{3,2,1,0:T(8,128)(2,1)S(1)}, bf16[1,1,128,1024]{3,2,1,0:T(8,128)(2,1)S(1)}, u32[]{:S(2)}, u32[]{:S(2)}) collective-permute-start(bf16[1,1,128,1024]{3,2,1,0:T(8,128)(2,1)S(1)} %fusion.51), channel_id=1, source_target_pairs={{0,2},{1,3},{2,0},{3,1},{4,6},{5,7},{6,4},{7,5},{8,10},{9,11},{10,... | collective-permute-start | bytes 786440 | tf_op jit(solution)/shard_map/ppermute | solution.py:59
  443.0 18.2 %collective-permute-start.100 = (bf16[1,2,128,1024]{3,2,1,0:T(8,128)(2,1)S(1)}, bf16[1,2,128,1024]{3,2,1,0:T(8,128)(2,1)S(1)}, u32[]{:S(2)}, u32[]{:S(2)}) collective-permute-start(bf16[1,2,128,1024]{3,2,1,0:T(8,128)(2,1)S(1)} %maximum_bitcast_fusion), channel_id=1, source_target_pairs={{0,2},{1,3},{2,0},{3,1},{4,6},{5,7},{6,4},{7,5},{8,10},{9,11},{10,... | collective-permute-start | bytes 1572872 | tf_op jit(solution)/shard_map/ppermute | solution.py:59
  445.1 19.5 %collective-permute-start.103 = (bf16[1,1,128,1024]{3,2,1,0:T(8,128)(2,1)S(1)}, bf16[1,1,128,1024]{3,2,1,0:T(8,128)(2,1)S(1)}, u32[]{:S(2)}, u32[]{:S(2)}) collective-permute-start(bf16[1,1,128,1024]{3,2,1,0:T(8,128)(2,1)S(1)} %fusion.50), channel_id=1, source_target_pairs={{0,2},{1,3},{2,0},{3,1},{4,6},{5,7},{6,4},{7,5},{8,10},{9,11},{10,... | collective-permute-start | bytes 786440 | tf_op jit(solution)/shard_map/ppermute | solution.py:59
  462.4 17.0 %collective-permute-start.101 = (bf16[2,2,128,1024]{3,2,1,0:T(8,128)(2,1)}, bf16[2,2,128,1024]{3,2,1,0:T(8,128)(2,1)}, u32[]{:S(2)}, u32[]{:S(2)}) collective-permute-start(bf16[2,2,128,1024]{3,2,1,0:T(8,128)(2,1)} %pad_maximum_fusion.9), channel_id=1, source_target_pairs={{0,1},{1,0},{2,3},{3,2},{4,5},{5,4},{6,7},{7,6},{8,9},{9,8},{10,11... | collective-permute-start | bytes 3145736 | tf_op jit(solution)/shard_map/ppermute | solution.py:59
  466.5 22.2 %collective-permute-start.98 = (bf16[2,128,1024]{2,1,0:T(8,128)(2,1)}, bf16[2,128,1024]{2,1,0:T(8,128)(2,1)}, u32[]{:S(2)}, u32[]{:S(2)}) collective-permute-start(bf16[2,128,1024]{2,1,0:T(8,128)(2,1)} %dynamic-slice_bitcast_fusion.4), channel_id=1, source_target_pairs={{0,8},{4,12},{8,0},{12,4},{16,24},{20,28},{24,16},{28,20},{1,9},{5... | collective-permute-start | bytes 1572872 | tf_op jit(solution)/shard_map/ppermute | solution.py:59
  492.2 14.5 %collective-permute-start.102 = (bf16[128,1024]{1,0:T(8,128)(2,1)S(1)}, bf16[128,1024]{1,0:T(8,128)(2,1)S(1)}, u32[]{:S(2)}, u32[]{:S(2)}) collective-permute-start(bf16[128,1024]{1,0:T(8,128)(2,1)S(1)} %dynamic-slice_bitcast_fusion.8), channel_id=1, source_target_pairs={{0,16},{4,20},{8,24},{12,28},{16,0},{20,4},{24,8},{28,12},{1,17},{... | collective-permute-start | bytes 786440 | tf_op jit(solution)/shard_map/ppermute | solution.py:59
  498.3 16.9 %collective-permute-start.110 = (bf16[2,1,128,1024]{3,2,1,0:T(8,128)(2,1)S(1)}, bf16[2,1,128,1024]{3,2,1,0:T(8,128)(2,1)S(1)}, u32[]{:S(2)}, u32[]{:S(2)}) collective-permute-start(bf16[2,1,128,1024]{3,2,1,0:T(8,128)(2,1)S(1)} %pad_maximum_fusion.19), channel_id=1, source_target_pairs={{0,1},{1,0},{2,3},{3,2},{4,5},{5,4},{6,7},{7,6},{8,9},{9,8},{10,11... | collective-permute-start | bytes 1572872 | tf_op jit(solution)/shard_map/ppermute | solution.py:59
  (190 other events, 1525.1 us)
Sparse Core Ops, SparseCore 0:
  73.1 65.5 all-gather.6
  140.9 54.7 all-gather.8
  197.8 49.4 all-gather.10
  268.5 103.6 reduce-scatter.1
